TPU v7x, 32 devices: a whole 2x2x4 slice. The times are simulated.
32 devices in a mesh: fsdp: 4 (over y, x), context: 4 (over z), tensor: 2 (over core).
Axes of the slice: x: 2, y: 2, z: 4, core: 2. Of those that a mesh axis runs over, the one named last changes fastest.
Arguments:
- tokens: bfloat16 [12288, 768], P(('fsdp', 'context')), may hold values from -6 to 6
- cotangent: bfloat16 [12288, 768], P(('fsdp', 'context')), may hold values from -6 to 6
- w_qkv: bfloat16 [3, 768, 768], P(None, 'fsdp', 'tensor'), may hold values from -0.21875 to 0.21875
- bias_qv: float32 [2, 768], P(None, 'tensor'), may hold values from -3 to 3
- w_attn_out: bfloat16 [768, 768], P('tensor', 'fsdp'), may hold values from -1.25 to 1.25
- w_up: bfloat16 [768, 3072], P('fsdp', 'tensor'), may hold values from -0.21875 to 0.21875
- bias_up: float32 [3072], P('tensor'), may hold values from -3 to 3
- w_down: bfloat16 [3072, 768], P('tensor', 'fsdp'), may hold values from -0.109375 to 0.109375
- gains: float32 [2, 768], replicated, may hold values from 0.1 to 1.9
- shifts: float32 [4, 768], replicated, may hold values from -3 to 3
- seq_lengths: int32 [4, 3], P('fsdp'), may hold values from 1 to 1536, 3072 in all within a row
- key_mask: int32 [12288], P('fsdp'), may hold values 0 or 1
Outputs:
- out: bfloat16 [12288, 768], P(('fsdp', 'context'))
- grad_tokens: bfloat16 [12288, 768], P(('fsdp', 'context'))
- grad_qkv: float32 [3, 768, 768], P(None, 'fsdp', 'tensor')
- grad_attn_out: float32 [768, 768], P('tensor', 'fsdp')
- grad_up: float32 [768, 3072], P('fsdp', 'tensor')
- grad_down: float32 [3072, 768], P('tensor', 'fsdp')
- grad_bias_qv: float32 [2, 768], P(None, 'tensor')
- grad_bias_up: float32 [3072], P('tensor')
- grad_gains: float32 [2, 768], replicated
- grad_shifts: float32 [4, 768], replicated
Inputs may be any that keep to these rules, and one draw needn't show every extreme that they name: `seq_lengths`: row f holds the lengths of the 3 sequences packed in order into the 3072 rows of group f; they sum to 3072 and the longest is 1536 in every row. `key_mask`: 1 marks a row that other rows of its sequence attend to; every row attends to itself.
All inputs are finite; a program needn't handle non-finite values. No bound on the sum of `key_mask` on one device may be relied on, other than what follows from the above.
Results may differ from a plain program's by a relative error of at most 0.022.
Values may be sent and summed in bfloat16 or wider, within the bound.
No kernel may reach another device: no remote copies, remote signals or barrier semaphores. Data moves between devices by JAX's collectives and lax.ppermute only.
A program may use at most 192 MiB of HBM per device.

v0:
```python
import jax
import jax.numpy as jnp
from jax import lax
from jax.sharding import PartitionSpec as P

EPSILON = 1e-12
SCORE_SCALE = 0.125
MASKED_SCORE = -1e30


def normalize(inputs):
    center = inputs - jnp.mean(inputs, axis=-1, keepdims=True)
    factor = lax.rsqrt(jnp.mean(center * center, axis=-1, keepdims=True) + EPSILON)
    return (center * factor, factor)


def norm_back(upstream, normed, factor, gain):
    scaled = upstream * gain
    return factor * (
        scaled
        - jnp.mean(scaled, axis=-1, keepdims=True)
        - normed * jnp.mean(scaled * normed, axis=-1, keepdims=True)
    )


def segment_ids(lengths_row, places):
    bounds = jnp.cumsum(lengths_row)
    return jnp.sum((places[:, None] >= bounds[None, :-1]).astype(jnp.int32), axis=1)


def split_heads(matrix, heads_here):
    return matrix.reshape(matrix.shape[0], heads_here, 64).transpose(1, 0, 2)


def join_heads(stacked):
    return stacked.transpose(1, 0, 2).reshape(stacked.shape[1], stacked.shape[0] * stacked.shape[2])


def score_grads(query_head, key_head, value_head, grad_head, log_head, delta_head, allowed):
    scores = (
        jnp.einsum("qd,kd->qk", query_head, key_head, preferred_element_type=jnp.float32)
        * SCORE_SCALE
    )
    probs = jnp.where(allowed, jnp.exp(scores - log_head[:, None]), 0.0)
    grad_prob = jnp.einsum("qd,kd->qk", grad_head, value_head, preferred_element_type=jnp.float32)
    grad_score = (probs * (grad_prob - delta_head[:, None])).astype(jnp.bfloat16)
    return (probs, grad_score)


def shards(
    tokens,
    cotangent,
    w_qkv,
    bias_qv,
    w_attn_out,
    w_up,
    bias_up,
    w_down,
    gains,
    shifts,
    seq_lengths,
    key_mask,
):
    row_count = tokens.shape[0]
    local_width = w_qkv.shape[2]
    heads_here = local_width // 64
    query_places = lax.axis_index("context") * row_count + jnp.arange(row_count, dtype=jnp.int32)
    lengths_row = seq_lengths[0]
    query_segment = segment_ids(lengths_row, query_places)

    def visible(length):
        key_places = jnp.arange(length, dtype=jnp.int32)
        key_segment = segment_ids(lengths_row, key_places)
        same = query_segment[:, None] == key_segment[None, :]
        return same & ((key_mask[None, :] == 1) | (query_places[:, None] == key_places[None, :]))

    w_proj, w_back, w_upper, w_lower = (
        lax.all_gather(w_qkv, "fsdp", axis=1, tiled=True),
        lax.all_gather(w_attn_out, "fsdp", axis=1, tiled=True),
        lax.all_gather(w_up, "fsdp", axis=0, tiled=True),
        lax.all_gather(w_down, "fsdp", axis=1, tiled=True),
    )
    projected = jnp.einsum("td,kde->kte", tokens, w_proj, preferred_element_type=jnp.float32)
    query = (projected[0] + bias_qv[0]).astype(jnp.bfloat16)
    key_rows = projected[1].astype(jnp.bfloat16)
    value_rows = (projected[2] + bias_qv[1]).astype(jnp.bfloat16)
    query_heads = split_heads(query, heads_here)
    start_state = (
        jnp.full((heads_here, row_count), MASKED_SCORE, jnp.float32),
        jnp.zeros((heads_here, row_count), jnp.float32),
        jnp.zeros((heads_here, row_count, 64), jnp.float32),
    )
    key_piece = lax.all_gather(key_rows, "context", axis=0, tiled=True)
    value_piece = lax.all_gather(value_rows, "context", axis=0, tiled=True)
    allowed = visible(key_piece.shape[0])

    def one_head(inputs):
        query_head, key_head, value_head, running_peak, running_total, running_sum = inputs
        scores = (
            jnp.einsum("qd,kd->qk", query_head, key_head, preferred_element_type=jnp.float32)
            * SCORE_SCALE
        )
        new_peak = jnp.maximum(
            running_peak, jnp.max(jnp.where(allowed, scores, MASKED_SCORE), axis=1)
        )
        weights = jnp.where(allowed, jnp.exp(scores - new_peak[:, None]), 0.0)
        fade = jnp.exp(running_peak - new_peak)
        new_total = running_total * fade + jnp.sum(weights, axis=1)
        new_sum = running_sum * fade[:, None] + jnp.dot(
            weights.astype(jnp.bfloat16), value_head, preferred_element_type=jnp.float32
        )
        return (new_peak, new_total, new_sum)

    peak, total, summed = lax.map(
        one_head,
        (
            query_heads,
            split_heads(key_piece, heads_here),
            split_heads(value_piece, heads_here),
            start_state[0],
            start_state[1],
            start_state[2],
        ),
    )
    attended = join_heads(summed / total[:, :, None]).astype(jnp.bfloat16)
    log_total = peak + jnp.log(total)
    branch_part = jnp.dot(attended, w_back, preferred_element_type=jnp.float32)
    first_sum = (
        tokens.astype(jnp.float32)
        + lax.psum(branch_part.astype(jnp.bfloat16), "tensor").astype(jnp.float32)
        + shifts[0]
    )
    normed1, factor1 = normalize(first_sum)
    first = normed1 * gains[0] + shifts[1]
    first_low = first.astype(jnp.bfloat16)
    upper = jnp.dot(first_low, w_upper, preferred_element_type=jnp.float32) + bias_up
    active_f, gelu_back = jax.vjp(lambda values: jax.nn.gelu(values, approximate=False), upper)
    active = active_f.astype(jnp.bfloat16)
    lower_part = jnp.dot(active, w_lower, preferred_element_type=jnp.float32)
    second_sum = (
        first + lax.psum(lower_part.astype(jnp.bfloat16), "tensor").astype(jnp.float32) + shifts[2]
    )
    normed2, factor2 = normalize(second_sum)
    out = (normed2 * gains[1] + shifts[3]).astype(jnp.bfloat16)
    upstream = cotangent.astype(jnp.float32)
    gain_two = jnp.sum(upstream * normed2, axis=0)
    shift_three = jnp.sum(upstream, axis=0)
    grad_second = norm_back(upstream, normed2, factor2, gains[1])
    shift_two = jnp.sum(grad_second, axis=0)
    lower_grad = grad_second.astype(jnp.bfloat16)
    grad_lower = jnp.einsum("tf,td->fd", active, lower_grad, preferred_element_type=jnp.float32)
    grad_active = jnp.einsum("td,fd->tf", lower_grad, w_lower, preferred_element_type=jnp.float32)
    grad_upper = gelu_back(grad_active)[0].astype(jnp.bfloat16)
    grad_bias_up = jnp.sum(grad_upper.astype(jnp.float32), axis=0)
    grad_upper_w = jnp.einsum(
        "td,tf->df", first_low, grad_upper, preferred_element_type=jnp.float32
    )
    back_part = jnp.einsum("tf,df->td", grad_upper, w_upper, preferred_element_type=jnp.float32)
    grad_first = grad_second + lax.psum(back_part.astype(jnp.bfloat16), "tensor").astype(
        jnp.float32
    )
    gain_one = jnp.sum(grad_first * normed1, axis=0)
    shift_one = jnp.sum(grad_first, axis=0)
    grad_first_sum = norm_back(grad_first, normed1, factor1, gains[0])
    shift_zero = jnp.sum(grad_first_sum, axis=0)
    branch_grad = grad_first_sum.astype(jnp.bfloat16)
    grad_back_w = jnp.einsum("te,td->ed", attended, branch_grad, preferred_element_type=jnp.float32)
    grad_attended = jnp.einsum(
        "td,ed->te", branch_grad, w_back, preferred_element_type=jnp.float32
    ).astype(jnp.bfloat16)
    grad_heads = split_heads(grad_attended, heads_here)
    delta = jnp.sum(
        grad_heads.astype(jnp.float32) * split_heads(attended, heads_here).astype(jnp.float32),
        axis=-1,
    )
    grad_query = jnp.zeros((heads_here, row_count, 64), jnp.float32)
    key_piece = lax.all_gather(key_rows, "context", axis=0, tiled=True)
    value_piece = lax.all_gather(value_rows, "context", axis=0, tiled=True)
    length = key_piece.shape[0]
    attend_allowed = visible(length)

    def one_head(inputs):
        query_head, key_head, value_head, grad_head, log_head, delta_head, grad_query_head = inputs
        probs, grad_score = score_grads(
            query_head, key_head, value_head, grad_head, log_head, delta_head, attend_allowed
        )
        grad_value = jnp.einsum(
            "qk,qd->kd", probs.astype(jnp.bfloat16), grad_head, preferred_element_type=jnp.float32
        )
        grad_query_head = (
            grad_query_head
            + jnp.einsum("qk,kd->qd", grad_score, key_head, preferred_element_type=jnp.float32)
            * SCORE_SCALE
        )
        grad_key = (
            jnp.einsum("qk,qd->kd", grad_score, query_head, preferred_element_type=jnp.float32)
            * SCORE_SCALE
        )
        return (grad_query_head, grad_key, grad_value)

    grad_query, key_terms, value_terms = lax.map(
        one_head,
        (
            query_heads,
            split_heads(key_piece, heads_here),
            split_heads(value_piece, heads_here),
            grad_heads,
            log_total,
            delta,
            grad_query,
        ),
    )
    grad_keys = join_heads(key_terms)
    grad_values = join_heads(value_terms)
    grad_keys_here, grad_values_here = (
        lax.psum_scatter(
            grad_keys.astype(jnp.bfloat16), "context", scatter_dimension=0, tiled=True
        ).astype(jnp.float32),
        lax.psum_scatter(
            grad_values.astype(jnp.bfloat16), "context", scatter_dimension=0, tiled=True
        ).astype(jnp.float32),
    )
    grad_query_low = join_heads(grad_query).astype(jnp.bfloat16)
    stacked = jnp.stack(
        [grad_query_low, grad_keys_here.astype(jnp.bfloat16), grad_values_here.astype(jnp.bfloat16)]
    )
    grad_proj = jnp.einsum("td,kte->kde", tokens, stacked, preferred_element_type=jnp.float32)
    grad_bias_qv = jnp.stack(
        [
            jnp.sum(stacked[0].astype(jnp.float32), axis=0),
            jnp.sum(stacked[2].astype(jnp.float32), axis=0),
        ]
    )
    input_part = jnp.einsum("kte,kde->td", stacked, w_proj, preferred_element_type=jnp.float32)
    grad_tokens = (
        grad_first_sum + lax.psum(input_part.astype(jnp.bfloat16), "tensor").astype(jnp.float32)
    ).astype(jnp.bfloat16)
    part_qkv, part_back, part_upper, part_lower = (
        lax.psum_scatter(
            grad_proj.astype(jnp.bfloat16), "fsdp", scatter_dimension=1, tiled=True
        ).astype(jnp.float32),
        lax.psum_scatter(
            grad_back_w.astype(jnp.bfloat16), "fsdp", scatter_dimension=1, tiled=True
        ).astype(jnp.float32),
        lax.psum_scatter(
            grad_upper_w.astype(jnp.bfloat16), "fsdp", scatter_dimension=0, tiled=True
        ).astype(jnp.float32),
        lax.psum_scatter(
            grad_lower.astype(jnp.bfloat16), "fsdp", scatter_dimension=1, tiled=True
        ).astype(jnp.float32),
    )
    share_qkv, share_back, share_upper, share_lower = (
        lax.psum(part_qkv.astype(jnp.bfloat16), "context").astype(jnp.float32),
        lax.psum(part_back.astype(jnp.bfloat16), "context").astype(jnp.float32),
        lax.psum(part_upper.astype(jnp.bfloat16), "context").astype(jnp.float32),
        lax.psum(part_lower.astype(jnp.bfloat16), "context").astype(jnp.float32),
    )
    gain_rows = jnp.stack([gain_one, gain_two])
    shift_rows = jnp.stack([shift_zero, shift_one, shift_two, shift_three])
    sum_bias_qv, sum_bias_up, sum_gains, sum_shifts = lax.psum(
        (grad_bias_qv, grad_bias_up, gain_rows, shift_rows), ("fsdp", "context")
    )
    return (
        out,
        grad_tokens,
        share_qkv,
        share_back,
        share_upper,
        share_lower,
        sum_bias_qv,
        sum_bias_up,
        sum_gains,
        sum_shifts,
    )


def solution(mesh):
    return jax.shard_map(
        shards,
        mesh=mesh,
        in_specs=(
            P(("fsdp", "context"), None),
            P(("fsdp", "context"), None),
            P(None, "fsdp", "tensor"),
            P(None, "tensor"),
            P("tensor", "fsdp"),
            P("fsdp", "tensor"),
            P("tensor"),
            P("tensor", "fsdp"),
            P(),
            P(),
            P("fsdp", None),
            P("fsdp"),
        ),
        out_specs=(
            P(("fsdp", "context"), None),
            P(("fsdp", "context"), None),
            P(None, "fsdp", "tensor"),
            P("tensor", "fsdp"),
            P("fsdp", "tensor"),
            P("tensor", "fsdp"),
            P(None, "tensor"),
            P("tensor"),
            P(),
            P(),
        ),
        check_vma=False,
    )
```

profile of v0, /device:TPU:0, one launch (start us, length us, event | category | flops | bytes accessed | tf_op | source)
XLA Modules:
  0.0 912.4 jit_solution(13213322940845944234)
XLA Ops:
  8.0 37.1 %all-gather.7.cloned.1.call-done = bf16[3,768,384]{2,1,0:T(8,128)(2,1)} async-done(((bf16[3,192,384]{2,1,0:T(8,128)(2,1)}), bf16[3,768,384]{2,1,0:T(8,128)(2,1)}) %all-gather.7.cloned.1.call-update) | async-done | bytes 1769488 | tf_op jit(solution)/shard_map/all_gather | solution.py:78
  45.1 3.4 convolution_bitcast_fusion
  54.5 10.9 %all_gather.23 = bf16[384,768]{0,1:T(8,128)(2,1)} all-gather(bf16[384,192]{0,1:T(8,128)(2,1)S(1)} %copy-done.28), channel_id=1, replica_groups=mesh['fsdp'=4,'context'=4,'tensor'=2] {'fsdp'}, dimensions={1}, use_global_device_ids=true | all-gather | bytes 737280 | tf_op jit(solution)/shard_map/all_gather | solution.py:79
  70.0 31.3 %all-gather.15.cloned.1.call-done = bf16[1,3072,384]{1,2,0:T(8,128)(2,1)} async-done(((bf16[1,768,384]{1,2,0:T(8,128)(2,1)}), bf16[1,3072,384]{1,2,0:T(8,128)(2,1)}) %all-gather.15.cloned.1.call-update) | async-done | bytes 2359312 | tf_op jit(solution)/shard_map/all_gather | solution.py:93
  101.3 5.7 copy.51
  107.0 45.2 %all-gather.9.cloned.1.call-done = bf16[3072,384]{0,1:T(8,128)(2,1)} async-done(((bf16[768,384]{0,1:T(8,128)(2,1)}), bf16[3072,384]{0,1:T(8,128)(2,1)}) %all-gather.9.cloned.1.call-update) | async-done | bytes 2359312 | tf_op jit(solution)/shard_map/all_gather | solution.py:94
  152.2 5.8 copy.52
  158.0 92.7 %while.32 = (s32[]{:T(128)}, f32[6,768]{1,0:T(8,128)S(1)}, f32[6,768]{1,0:T(8,128)S(1)}, f32[6,768,64]{1,2,0:T(8,128)S(1)}, bf16[6,768,64]{2,1,0:T(8,128)(2,1)},...) while((s32[]{:T(128)}, f32[6,768]{1,0:T(8,128)S(1)}, ...), condition=%wide.region_6.7_spmd.clone.clone, body=%wide.region_3.6_spmd.clone.sunk.clone | while | flops 658295808 | bytes 30400636 | solution.py:114
  158.1 5.0 select_reduce_fusion.3
  163.1 4.8 fusion.154
  167.9 5.4 fusion.155
  173.5 5.0 select_reduce_fusion.3
  178.5 4.8 fusion.154
  183.4 5.4 fusion.155
  189.0 5.0 select_reduce_fusion.3
  194.0 4.8 fusion.154
  198.8 5.4 fusion.155
  204.4 5.0 select_reduce_fusion.3
  209.4 4.8 fusion.154
  214.2 5.4 fusion.155
  219.8 5.0 select_reduce_fusion.3
  224.8 4.8 fusion.154
  229.7 5.4 fusion.155
  235.3 5.0 select_reduce_fusion.3
  240.3 4.8 fusion.154
  245.1 5.4 fusion.155
  255.9 17.1 %all-reduce.8.cloned.1.call-done = bf16[768,768]{1,0:T(8,128)(2,1)} async-done(((bf16[768,768]{1,0:T(8,128)(2,1)}), bf16[768,768]{1,0:T(8,128)(2,1)}) %all-reduce.8.cloned.1.call-update) | async-done | bytes 1179664 | tf_op jit(solution)/shard_map/psum | solution.py:130
  275.5 37.7 %all-gather.11.cloned.1.call-done = bf16[768,1536]{1,0:T(8,128)(2,1)} async-done(((bf16[192,1536]{1,0:T(8,128)(2,1)}), bf16[768,1536]{1,0:T(8,128)(2,1)}) %all-gather.11.cloned.1.call-update) | async-done | bytes 2359312 | tf_op jit(solution)/shard_map/all_gather | solution.py:80
  313.3 15.5 %multiply_convert_fusion.1 = (bf16[768,1536]{1,0:T(8,128)(2,1)}, f32[768,1536]{1,0:T(8,128)}, f32[768,1536]{1,0:T(8,128)}) fusion(f32[1536]{0:T(1024)S(1)} %copy-done.48, bf16[768,1536]{1,0:T(8,128)(2,1)} %all-gather.11.cloned.1.call-done, f32[768]{0:T(1024)S(1)} %get-tuple-element.273, f32[768]{0:T(1024)S(1)} %get-tuple-element.277, ...), kind=kOutput, calls=%fused_computation.67 | convolution fusion | flops 1895104512 | bytes 16536576 | tf_op jit(solution)/shard_map/dot_general | solution.py:136
  328.7 23.6 %all-gather.13.cloned.1.call-done = bf16[1536,768]{0,1:T(8,128)(2,1)} async-done(((bf16[1536,192]{0,1:T(8,128)(2,1)}), bf16[1536,768]{0,1:T(8,128)(2,1)}) %all-gather.13.cloned.1.call-update) | async-done | bytes 2359312 | tf_op jit(solution)/shard_map/all_gather | solution.py:81
  352.3 5.4 convolution_convert_fusion.4
  357.8 19.8 %all-reduce.10.cloned.1.call-done = bf16[768,768]{1,0:T(8,128)(2,1)} async-done(((bf16[768,768]{1,0:T(8,128)(2,1)}), bf16[768,768]{1,0:T(8,128)(2,1)}) %all-reduce.10.cloned.1.call-update) | async-done | bytes 1179664 | tf_op jit(solution)/shard_map/psum | solution.py:141
  384.8 7.2 convert_reduce_fusion
  398.3 19.3 %all-reduce.12.cloned.1.call-done = bf16[768,768]{1,0:T(8,128)(2,1)} async-done(((bf16[768,768]{1,0:T(8,128)(2,1)}), bf16[768,768]{1,0:T(8,128)(2,1)}) %all-reduce.12.cloned.1.call-update) | async-done | bytes 1179664 | tf_op jit(solution)/shard_map/psum | solution.py:159
  417.6 3.9 multiply_reduce_fusion
  426.4 106.2 %while.33 = (s32[]{:T(128)}, bf16[6,768,64]{1,2,0:T(8,128)(2,1)}, bf16[6,3072,64]{1,2,0:T(8,128)(2,1)}, bf16[6,3072,64]{1,2,0:T(8,128)(2,1)}, bf16[6,768,64]{2,1...) while((s32[]{:T(128)}, bf16[6,768,64]{1,2,0:T(8,128)(2,1)}, ...), condition=%wide.region_20.21_spmd.clone.clone, body=%wide.region_19.20_spmd.clone.sunk.clone | while | flops 1536147456 | bytes 51950792 | solution.py:201
  427.2 5.4 exponential_select_fusion.4
  435.2 3.3 multiply_convert_fusion.4
  444.9 5.4 exponential_select_fusion.4
  452.9 3.3 multiply_convert_fusion.4
  462.6 5.4 exponential_select_fusion.4
  470.6 3.3 multiply_convert_fusion.4
  480.3 5.4 exponential_select_fusion.4
  488.3 3.3 multiply_convert_fusion.4
  498.0 5.4 exponential_select_fusion.4
  506.0 3.3 multiply_convert_fusion.4
  515.7 5.4 exponential_select_fusion.4
  523.7 3.3 multiply_convert_fusion.4
  532.6 4.3 copy.54
  537.0 4.3 copy.55
  543.7 42.3 %reduce-scatter.9.cloned.1.call-done = bf16[768,384]{1,0:T(8,128)(2,1)} async-done(((bf16[3072,384]{1,0:T(8,128)(2,1)}), bf16[768,384]{1,0:T(8,128)(2,1)}) %reduce-scatter.9.cloned.1.call-update) | async-done | bytes 589840 | tf_op jit(solution)/shard_map/reduce_scatter | solution.py:216
  586.0 49.3 %reduce-scatter.11.cloned.1.call-done = bf16[768,384]{1,0:T(8,128)(2,1)} async-done(((bf16[3072,384]{1,0:T(8,128)(2,1)}), bf16[768,384]{1,0:T(8,128)(2,1)}) %reduce-scatter.11.cloned.1.call-update) | async-done | bytes 589840 | tf_op jit(solution)/shard_map/reduce_scatter | solution.py:219
  635.3 4.2 convert_bitcast_fusion
  639.5 5.2 copy.60
  644.7 3.2 copy.63
  650.7 5.9 convolution_convert_fusion
  657.4 5.9 convolution_convert_fusion.1
  664.5 4.4 bitcast_convert_fusion
  669.1 10.8 %reduce-scatter.19.cloned.1.call-done = bf16[192,1152]{1,0:T(8,128)(2,1)} async-done(((bf16[768,1152]{1,0:T(8,128)(2,1)}), bf16[192,1152]{1,0:T(8,128)(2,1)}) %reduce-scatter.19.cloned.1.call-update) | async-done | bytes 442384
  682.6 26.1 %reduce-scatter.13.cloned.1.call-done = bf16[384,192]{0,1:T(8,128)(2,1)} async-done(((bf16[384,768]{0,1:T(8,128)(2,1)}), bf16[384,192]{0,1:T(8,128)(2,1)}) %reduce-scatter.13.cloned.1.call-update) | async-done | bytes 147472 | tf_op jit(solution)/shard_map/reduce_scatter | solution.py:242
  708.7 40.4 %reduce-scatter.17.cloned.1.call-done = bf16[1536,192]{0,1:T(8,128)(2,1)} async-done(((bf16[1536,768]{0,1:T(8,128)(2,1)}), bf16[1536,192]{0,1:T(8,128)(2,1)}) %reduce-scatter.17.cloned.1.call-update) | async-done | bytes 589840 | tf_op jit(solution)/shard_map/reduce_scatter | solution.py:248
  749.1 40.3 %reduce-scatter.15.cloned.1.call-done = bf16[192,1536]{1,0:T(8,128)(2,1)} async-done(((bf16[768,1536]{1,0:T(8,128)(2,1)}), bf16[192,1536]{1,0:T(8,128)(2,1)}) %reduce-scatter.15.cloned.1.call-update) | async-done | bytes 589840 | tf_op jit(solution)/shard_map/reduce_scatter | solution.py:245
  795.0 79.4 %all-reduce = (f32[2,384]{1,0:T(2,128)}, f32[1536]{0:T(1024)}, f32[2,768]{1,0:T(2,128)}, f32[4,768]{1,0:T(4,128)}) all-reduce(f32[2,384]{1,0:T(2,128)S(1)} %pad_maximum_fusion.5, f32[1536]{0:T(1024)} %get-tuple-element.353, f32[2,768]{1,0:T(2,128)S(1)} %pad_maximum_fusion.4, ...), channel_id=1, replica_groups=mesh['fsdp'=4,'context'=4,'tensor'=2] {'fsdp','context'}, use_global_device_ids=true, to_apply=%region_34.35 | all-reduce | flops 6912 | bytes 55296 | tf_op jit(solution)/shard_map/psum | solution.py:260
  877.0 21.2 %all-reduce.16.cloned.1.call-done = (bf16[3,192,384]{1,2,0:T(8,128)(2,1)}, bf16[384,192]{0,1:T(8,128)(2,1)}, bf16[192,1536]{1,0:T(8,128)(2,1)}, bf16[1536,192]{0,1:T(8,128)(2,1)}) async-done(((bf16[3,192,384]{1,2,0:T(8,128)(2,1)}, bf16[384,192]{0,1:T(8,128)(2,1)}, bf16[192,1536]{1,0:T(8,128)(2,1)}, bf16[1536,192]{0,1:T(8,128)(2,1)}), (bf16[3,192,384]{1,2,0:T(8,128)(2,1)}, bf16[384,192]{0,1:T(8,128)(2,1)}, ...) | async-done | bytes 1769488 | tf_op jit(solution)/shard_map/psum | solution.py:253
  (273 shorter events, 117.9 us)
Async XLA Ops:
  7.2 37.9 %all-gather.7.cloned.1.call-start = ((), (), s32[]{:S(2)}) async-start(), calls=%async_computation.6 | async-start | bytes 2211840 | tf_op jit(solution)/shard_map/all_gather | solution.py:78
  7.9 43.3 %copy-start.45 = (f32[2,384]{1,0:T(2,128)S(1)}, f32[2,384]{1,0:T(2,128)}, u32[]{:S(2)}) copy-start(f32[2,384]{1,0:T(2,128)} %param.19) | copy-start | bytes 9220
  7.9 93.3 %all-gather.15.cloned.1.call-start = ((), (), s32[]{:S(2)}) async-start(), calls=%async_computation.19 | async-start | bytes 2949120 | tf_op jit(solution)/shard_map/all_gather | solution.py:93
  50.2 3.4 copy-start.49
  50.2 4.3 copy-start.28
  50.2 16.0 %copy-start.43 = (s32[3072]{0:T(1024)S(1)}, s32[3072]{0:T(1024)}, u32[]{:S(2)}) copy-start(s32[3072]{0:T(1024)} %param.27) | copy-start | bytes 36868
  51.1 101.1 %all-gather.9.cloned.1.call-start = ((), (), s32[]{:S(2)}) async-start(), calls=%async_computation.7 | async-start | bytes 2949120 | tf_op jit(solution)/shard_map/all_gather | solution.py:94
  51.2 15.6 %slice-start = ((f32[3,768,384]{1,2,0:T(8,128)}), f32[1,768,384]{1,2,0:T(8,128)S(1)}, s32[]{:S(2)}) async-start(f32[3,768,384]{1,2,0:T(8,128)} %copy-done.13), calls=%async_computation.22 | async-start | bytes 2359296 | tf_op jit(solution)/shard_map/slice | solution.py:84
  53.6 219.4 %all-reduce.8.cloned.1.call-start = ((), (), s32[]{:S(2)}) async-start(), calls=%async_computation.8 | async-start | bytes 2359296 | tf_op jit(solution)/shard_map/psum | solution.py:130
  152.2 5.8 copy-start.14
  152.2 5.8 copy-start.22
  152.2 5.8 copy-start.25
  152.2 5.8 copy-start.29
  152.2 5.8 copy-start.36
  158.0 94.5 %copy-start.7 = (bf16[384,768]{0,1:T(8,128)(2,1)S(1)}, bf16[384,768]{0,1:T(8,128)(2,1)}, u32[]{:S(2)}) copy-start(bf16[384,768]{0,1:T(8,128)(2,1)} %all_gather.23) | copy-start | bytes 1769476
  250.7 146.9 %copy-start.23 = (f32[6,768]{1,0:T(8,128)}, f32[6,768]{1,0:T(8,128)S(1)}, u32[]{:S(2)}) copy-start(f32[6,768]{1,0:T(8,128)S(1)} %get-tuple-element.114) | copy-start | bytes 55300
  252.6 3.3 copy-start.44
  252.6 3.3 copy-start.42
  252.6 20.4 %copy-start = (bf16[768,768]{1,0:T(8,128)(2,1)S(1)}, bf16[768,768]{1,0:T(8,128)(2,1)}, u32[]{:S(2)}) copy-start(bf16[768,768]{1,0:T(8,128)(2,1)} %param.16) | copy-start | bytes 3538948
  254.4 58.8 %all-gather.11.cloned.1.call-start = ((), (), s32[]{:S(2)}) async-start(), calls=%async_computation.9 | async-start | bytes 2949120 | tf_op jit(solution)/shard_map/all_gather | solution.py:80
  255.0 97.3 %all-gather.13.cloned.1.call-start = ((), (), s32[]{:S(2)}) async-start(), calls=%async_computation.10 | async-start | bytes 2949120 | tf_op jit(solution)/shard_map/all_gather | solution.py:81
  255.6 122.0 %all-reduce.10.cloned.1.call-start = ((), (), s32[]{:S(2)}) async-start(), calls=%async_computation.11 | async-start | bytes 2359296 | tf_op jit(solution)/shard_map/psum | solution.py:141
  255.9 161.7 %copy-start.32 = (f32[768]{0:T(1024)}, f32[768]{0:T(1024)S(1)}, u32[]{:S(2)}) copy-start(f32[768]{0:T(1024)S(1)} %get-tuple-element.277) | copy-start | bytes 9220
  255.9 121.7 %copy-start.37 = (f32[768]{0:T(1024)}, f32[768]{0:T(1024)S(1)}, u32[]{:S(2)}) copy-start(f32[768]{0:T(1024)S(1)} %get-tuple-element.273) | copy-start | bytes 9220
  255.9 161.6 %copy-start.26 = (f32[768]{0:T(1024)}, f32[768]{0:T(1024)S(1)}, u32[]{:S(2)}) copy-start(f32[768]{0:T(1024)S(1)} %get-tuple-element.274) | copy-start | bytes 9220
  273.0 1.8 copy-start.1
  273.0 40.3 %copy-start.48 = (f32[1536]{0:T(1024)S(1)}, f32[1536]{0:T(1024)}, u32[]{:S(2)}) copy-start(f32[1536]{0:T(1024)} %param.22) | copy-start | bytes 18436
  274.8 142.7 %copy-start.30 = (f32[768]{0:T(1024)}, f32[768]{0:T(1024)S(1)}, u32[]{:S(2)}) copy-start(f32[768]{0:T(1024)S(1)} %broadcast_multiply_fusion.5) | copy-start | bytes 9220
  275.5 142.0 %copy-start.34 = (f32[768]{0:T(1024)}, f32[768]{0:T(1024)S(1)}, u32[]{:S(2)}) copy-start(f32[768]{0:T(1024)S(1)} %add_rsqrt_fusion.1) | copy-start | bytes 9220
  357.8 59.8 %all-reduce.12.cloned.1.call-start = ((), (), s32[]{:S(2)}) async-start(), calls=%async_computation.12 | async-start | bytes 2359296 | tf_op jit(solution)/shard_map/psum | solution.py:159
  382.9 1.9 copy-start.47
  384.8 7.3 copy-start.3
  384.8 8.6 copy-start.46
  396.5 189.5 %reduce-scatter.9.cloned.1.call-start = ((), (), s32[]{:S(2)}) async-start(), calls=%async_computation.13 | async-start | bytes 2949120 | tf_op jit(solution)/shard_map/reduce_scatter | solution.py:216
  417.6 4.0 copy-start.2
  417.6 4.0 copy-start.4
  417.6 4.0 copy-start.12
  421.5 2.8 copy-start.8
  435.2 3.3 copy-start.9
  441.2 2.9 copy-start.10
  452.9 3.3 copy-start.9
  458.9 2.9 copy-start.10
  470.6 3.3 copy-start.9
  476.6 2.9 copy-start.10
  488.3 3.3 copy-start.9
  494.3 2.9 copy-start.10
  506.0 3.3 copy-start.9
  512.0 2.9 copy-start.10
  523.7 3.3 copy-start.9
  529.7 2.9 copy-start.10
  536.9 98.3 %reduce-scatter.11.cloned.1.call-start = ((), (), s32[]{:S(2)}) async-start(), calls=%async_computation.14 | async-start | bytes 2949120 | tf_op jit(solution)/shard_map/reduce_scatter | solution.py:219
  541.3 138.6 %reduce-scatter.19.cloned.1.call-start = ((), (), s32[]{:S(2)}) async-start(), calls=%async_computation.20 | async-start | bytes 2211840
  647.9 60.8 %reduce-scatter.13.cloned.1.call-start = ((), (), s32[]{:S(2)}) async-start(), calls=%async_computation.16 | async-start | bytes 737280 | tf_op jit(solution)/shard_map/reduce_scatter | solution.py:242
  650.7 98.4 %reduce-scatter.17.cloned.1.call-start = ((), (), s32[]{:S(2)}) async-start(), calls=%async_computation.18 | async-start | bytes 2949120 | tf_op jit(solution)/shard_map/reduce_scatter | solution.py:248
  656.7 132.8 %reduce-scatter.15.cloned.1.call-start = ((), (), s32[]{:S(2)}) async-start(), calls=%async_computation.17 | async-start | bytes 2949120 | tf_op jit(solution)/shard_map/reduce_scatter | solution.py:245
  663.3 211.1 %all-reduce.14.cloned.1.call-start = ((), (), s32[]{:S(2)}) async-start(), calls=%async_computation.15 | async-start | bytes 2359296 | tf_op jit(solution)/shard_map/psum | solution.py:236
  669.0 123.0 %copy-start.40 = (f32[768]{0:T(1024)S(1)}, f32[768]{0:T(1024)}, u32[]{:S(2)}) copy-start(f32[768]{0:T(1024)} %get-tuple-element.263) | copy-start | bytes 9220
  669.0 123.6 %copy-start.39 = (f32[768]{0:T(1024)S(1)}, f32[768]{0:T(1024)}, u32[]{:S(2)}) copy-start(f32[768]{0:T(1024)} %get-tuple-element.268) | copy-start | bytes 9220
  669.0 123.6 %copy-start.38 = (f32[768]{0:T(1024)S(1)}, f32[768]{0:T(1024)}, u32[]{:S(2)}) copy-start(f32[768]{0:T(1024)} %get-tuple-element.269) | copy-start | bytes 9220
  669.0 123.6 %copy-start.41 = (f32[768]{0:T(1024)S(1)}, f32[768]{0:T(1024)}, u32[]{:S(2)}) copy-start(f32[768]{0:T(1024)} %get-tuple-element.338) | copy-start | bytes 9220
  669.0 124.2 %copy-start.11 = (bf16[6,768,64]{1,2,0:T(8,128)(2,1)S(1)}, bf16[6,768,64]{1,2,0:T(8,128)(2,1)}, u32[]{:S(2)}) copy-start(bf16[6,768,64]{1,2,0:T(8,128)(2,1)} %get-tuple-element.116) | copy-start | bytes 1769476
  669.0 229.1 %all-reduce.16.cloned.1.call-start = ((), (), s32[]{:S(2)}) async-start(), calls=%async_computation.21 | async-start | bytes 3833856 | tf_op jit(solution)/shard_map/psum | solution.py:253
  682.6 112.2 %copy-start.20 = (bf16[768,384]{1,0:T(8,128)(2,1)S(1)}, bf16[768,384]{1,0:T(8,128)(2,1)}, u32[]{:S(2)}) copy-start(bf16[768,384]{1,0:T(8,128)(2,1)} %reduce-scatter.11.cloned.1.call-done) | copy-start | bytes 1769476
  898.2 6.1 copy-start.18
  (14 other events, 15.3 us)
Sparse Core Ops, SparseCore 0:
  9.8 35.1 all-gather.6
  51.2 49.9 all-gather.14
  103.4 48.7 all-gather.8
  254.5 18.4 all-reduce.7
  274.7 38.5 all-gather.10
  314.9 37.3 all-gather.12
  357.9 19.6 all-reduce.9
  396.6 20.8 all-reduce.11
  537.1 48.8 reduce-scatter.8
  588.1 47.1 reduce-scatter.10
  648.0 31.8 reduce-scatter.18
  683.2 25.4 reduce-scatter.12
  711.7 37.3 reduce-scatter.16
  752.0 37.3 reduce-scatter.14
  792.2 19.6 all-reduce.13
  814.9 83.1 all-reduce.15
where the time goes:
time: 918 us; the launch traced here: 912 us
  waiting for transfers between devices  463 us (50%)
  matrix products  224 us (24%)
  blocking collectives  90.3 us (10%)
  other arithmetic  62 us (7%)
  local copies, waits for them, and re-layouts  56.2 us (6%)
  between operations  14.9 us (2%)
    psum x1, blocking collectives, shards(): lax.psum((grad_bias_qv, grad_bias_up, gain_rows, shift_rows), ('fsdp', 'c...  79.4 us
    reduce_scatter x1, waiting for transfers between devices, shards(): lax.psum_scatter(grad_values.astype(jnp.bfloat16), 'context', scatter_dim...  49.3 us
    all_gather x1, waiting for transfers between devices, shards(): value_piece = lax.all_gather(value_rows, 'context', axis=0, tiled=True)  45.2 us
    reduce_scatter x1, waiting for transfers between devices, shards(): lax.psum_scatter(grad_keys.astype(jnp.bfloat16), 'context', scatter_dimen...  42.3 us
    reduce_scatter x1, waiting for transfers between devices, shards(): lax.psum_scatter(grad_lower.astype(jnp.bfloat16), 'fsdp', scatter_dimensi...  40.4 us
    reduce_scatter x1, waiting for transfers between devices, shards(): lax.psum_scatter(grad_upper_w.astype(jnp.bfloat16), 'fsdp', scatter_dimen...  40.3 us
    all_gather x1, waiting for transfers between devices, shards(): lax.all_gather(w_up, 'fsdp', axis=0, tiled=True)  37.7 us
    all_gather x1, waiting for transfers between devices, shards(): lax.all_gather(w_qkv, 'fsdp', axis=1, tiled=True)  37.1 us
  transfers between devices with their start and end apart: 16, of which 15 were waited for; matrix products, arithmetic and copies ran while one was open for 8% of the time, Pallas kernels for 0%

commit v1 on v0

v1 whole, which is shorter than its diff:
```python
import jax
import jax.numpy as jnp
import numpy as np
from jax import lax
from jax.experimental import pallas as pl
from jax.experimental.pallas import tpu as pltpu
from jax.sharding import PartitionSpec as P

EPSILON = 1e-12
LOG2E = 1.4426950408889634
NEG = -1e30
BQ = 256
BK = 256
F32 = jnp.float32
BF16 = jnp.bfloat16
ROW = (((1,), (1,)), ((), ()))
COL = (((1,), (0,)), ((), ()))
LIMIT = 56 * 1024 * 1024
COST = pl.CostEstimate(flops=36_000_000_000, transcendentals=0, bytes_accessed=8_000_000)
PAIR_COST = pl.CostEstimate(flops=14_000_000_000, transcendentals=0, bytes_accessed=4_000_000)


def dot(a, b, dims=COL):
    return lax.dot_general(a, b, dims, preferred_element_type=F32)


def normalize(inputs):
    center = inputs - jnp.mean(inputs, axis=-1, keepdims=True)
    factor = lax.rsqrt(jnp.mean(center * center, axis=-1, keepdims=True) + EPSILON)
    return (center * factor, factor)


def norm_back(upstream, normed, factor, gain):
    scaled = upstream * gain
    return factor * (
        scaled
        - jnp.mean(scaled, axis=-1, keepdims=True)
        - normed * jnp.mean(scaled * normed, axis=-1, keepdims=True)
    )


def segment_of(places, b1, b2):
    return (places >= b1).astype(jnp.int32) + (places >= b2).astype(jnp.int32)


def key_range(first, last, b1, b2, total):
    lo = jnp.where(first >= b2, b2, jnp.where(first >= b1, b1, 0))
    hi = jnp.where(last >= b2, total, jnp.where(last >= b1, b2, b1))
    return lo, hi


def half_mask(rows, side):
    lane = lax.broadcasted_iota(jnp.int32, (rows, 128), 1)
    return (lane < 64) if side == 0 else (lane >= 64)


def pick(pair, side):
    return jnp.where(half_mask(pair.shape[0], side), pair, jnp.zeros_like(pair))


def fill_bias(bias_ref, kb_ref, first, b1, b2, j0, j1):
    rows = first + lax.broadcasted_iota(jnp.int32, (BQ, 1), 0)
    row_seg = segment_of(rows, b1, b2)

    def body(j, carry):
        cols = j * BK + lax.broadcasted_iota(jnp.int32, (1, BK), 1)
        col_seg = segment_of(cols, b1, b2)
        kept = jnp.where(rows == cols, 0.0, jnp.broadcast_to(kb_ref[j], (BQ, BK)))
        bias_ref[j] = jnp.where(row_seg == col_seg, kept, NEG)
        return carry

    lax.fori_loop(j0, j1, body, 0)


def attend_kernel(s_ref, q_ref, k_ref, v_ref, kb_ref, o_ref, lse_ref, lset_ref, score, bias):
    total = k_ref.shape[0]
    pairs = q_ref.shape[1] // 128
    b1, b2 = s_ref[0], s_ref[1]
    first = s_ref[2] + pl.program_id(0) * BQ
    lo, hi = key_range(first, first + BQ - 1, b1, b2, total)
    j0, j1 = lo // BK, (hi + BK - 1) // BK
    fill_bias(bias, kb_ref, first, b1, b2, j0, j1)
    lane = lax.broadcasted_iota(jnp.int32, (BQ, 128), 1)
    lse_all = jnp.zeros((BQ, 128), F32)
    heads = 2 * pairs
    peak = None
    held = None
    for h in range(-1, heads):
        nxt = h + 1
        if nxt < heads:
            np_, ns = nxt // 2, nxt % 2
            q_head = pick(q_ref[:, np_ * 128 : np_ * 128 + 128], ns)
        if h >= 0:
            cp = h // 2

        def body(j, carry):
            top, tot, acc = carry
            rows = pl.ds(pl.multiple_of(j * BK, BK), BK)
            if nxt < heads:
                s = dot(q_head, k_ref[rows, np_ * 128 : np_ * 128 + 128], ROW) + bias[j]
                score[nxt % 2, j] = s
                top = jnp.maximum(top, jnp.maximum(s[:, :128], s[:, 128:]))
            if h >= 0:
                p = jnp.exp2(score[h % 2, j] - peak)
                tot = tot + (p[:, :128] + p[:, 128:])
                acc = acc + dot(p.astype(BF16), v_ref[rows, cp * 128 : cp * 128 + 128])
            return (top, tot, acc)

        start = (jnp.full((BQ, 128), NEG, F32), jnp.zeros((BQ, 128), F32), jnp.zeros((BQ, 128), F32))
        top, tot, acc = lax.fori_loop(j0, j1, body, start)
        if h >= 0:
            whole = jnp.sum(tot, axis=1, keepdims=True)
            result = acc / whole
            lse_all = jnp.where(lane == h, peak + jnp.log2(whole), lse_all)
            if h % 2 == 0:
                held = result
            else:
                o_ref[:, cp * 128 : cp * 128 + 128] = jnp.where(lane < 64, held, result).astype(BF16)
        peak = jnp.max(top, axis=1, keepdims=True)
    lse_ref[...] = lse_all
    lset_ref[...] = jnp.transpose(lse_all)[: lset_ref.shape[0], :]


def attend(scalars, qkv, kb, rows, pairs):
    total = qkv.shape[0]
    width = pairs * 128
    return pl.pallas_call(
        attend_kernel,
        grid_spec=pltpu.PrefetchScalarGridSpec(
            num_scalar_prefetch=1,
            grid=(rows // BQ,),
            in_specs=[
                pl.BlockSpec((BQ, width), lambda i, s: (s[2] // BQ + i, 0)),
                pl.BlockSpec((total, width), lambda i, s: (0, 1), pipeline_mode=pl.Buffered(1)),
                pl.BlockSpec((total, width), lambda i, s: (0, 2), pipeline_mode=pl.Buffered(1)),
                pl.BlockSpec((total // BK, 1, BK), lambda i, s: (0, 0, 0)),
            ],
            out_specs=[
                pl.BlockSpec((BQ, width), lambda i, s: (i, 0)),
                pl.BlockSpec((BQ, 128), lambda i, s: (i, 0)),
                pl.BlockSpec((8, BQ), lambda i, s: (0, i)),
            ],
            scratch_shapes=[
                pltpu.VMEM((2, total // BK, BQ, BK), F32),
                pltpu.VMEM((total // BK, BQ, BK), F32),
            ],
        ),
        out_shape=[
            jax.ShapeDtypeStruct((rows, width), BF16),
            jax.ShapeDtypeStruct((rows, 128), F32),
            jax.ShapeDtypeStruct((8, rows), F32),
        ],
        compiler_params=pltpu.CompilerParams(
            dimension_semantics=("arbitrary",), vmem_limit_bytes=LIMIT
        ),
        cost_estimate=COST,
        name="attend",
    )(scalars, qkv, qkv, qkv, kb)


def query_kernel(s_ref, q_ref, k_ref, v_ref, do_ref, o_ref, lse_ref, kb_ref, dq_ref, bias):
    total = k_ref.shape[0]
    pairs = q_ref.shape[1] // 128
    b1, b2 = s_ref[0], s_ref[1]
    first = s_ref[2] + pl.program_id(0) * BQ
    lo, hi = key_range(first, first + BQ - 1, b1, b2, total)
    j0, j1 = lo // BK, (hi + BK - 1) // BK
    fill_bias(bias, kb_ref, first, b1, b2, j0, j1)
    low = half_mask(BQ, 0)
    for p in range(pairs):
        span = slice(p * 128, p * 128 + 128)
        grads = do_ref[:, span]
        product = grads.astype(F32) * o_ref[:, span].astype(F32)
        sides = []
        for side in range(2):
            h = 2 * p + side
            sides.append(
                (
                    pick(q_ref[:, span], side),
                    pick(grads, side),
                    jnp.sum(pick(product, side), axis=1, keepdims=True),
                    lse_ref[:, h : h + 1],
                )
            )

        def body(j, accs):
            rows = pl.ds(pl.multiple_of(j * BK, BK), BK)
            keys = k_ref[rows, span]
            values = v_ref[rows, span]
            out = []
            for (qh, gh, delta, lse), acc in zip(sides, accs):
                prob = jnp.exp2(dot(qh, keys, ROW) + bias[j] - lse)
                score = (prob * (dot(gh, values, ROW) - delta)).astype(BF16)
                out.append(acc + dot(score, keys))
            return tuple(out)

        zero = jnp.zeros((BQ, 128), F32)
        left, right = lax.fori_loop(j0, j1, body, (zero, zero))
        dq_ref[:, span] = (jnp.where(low, left, right) * 0.125).astype(BF16)


def query_grads(scalars, qkv, dout, att, lse, kb, rows, pairs):
    total = qkv.shape[0]
    width = pairs * 128
    return pl.pallas_call(
        query_kernel,
        grid_spec=pltpu.PrefetchScalarGridSpec(
            num_scalar_prefetch=1,
            grid=(rows // BQ,),
            in_specs=[
                pl.BlockSpec((BQ, width), lambda i, s: (s[2] // BQ + i, 0)),
                pl.BlockSpec((total, width), lambda i, s: (0, 1), pipeline_mode=pl.Buffered(1)),
                pl.BlockSpec((total, width), lambda i, s: (0, 2), pipeline_mode=pl.Buffered(1)),
                pl.BlockSpec((BQ, width), lambda i, s: (i, 0)),
                pl.BlockSpec((BQ, width), lambda i, s: (i, 0)),
                pl.BlockSpec((BQ, 128), lambda i, s: (i, 0)),
                pl.BlockSpec((total // BK, 1, BK), lambda i, s: (0, 0, 0)),
            ],
            out_specs=pl.BlockSpec((BQ, width), lambda i, s: (i, 0)),
            scratch_shapes=[pltpu.VMEM((total // BK, BQ, BK), F32)],
        ),
        out_shape=jax.ShapeDtypeStruct((rows, width), BF16),
        compiler_params=pltpu.CompilerParams(
            dimension_semantics=("arbitrary",), vmem_limit_bytes=LIMIT
        ),
        cost_estimate=COST,
        name="query_grads",
    )(scalars, qkv, qkv, qkv, dout, att, lse, kb)


def key_kernel(s_ref, k_ref, v_ref, q_ref, do_ref, stat_ref, mask_ref, dk_ref, dv_ref, *, pair, per):
    total = q_ref.shape[0]
    b1, b2 = s_ref[0], s_ref[1]
    first = s_ref[2] + pl.program_id(0) * BK
    lo, hi = key_range(first, first + BK - 1, b1, b2, total)
    j0, j1 = lo // BQ, (hi + BQ - 1) // BQ
    rows = first + lax.broadcasted_iota(jnp.int32, (BK, 1), 0)
    row_seg = segment_of(rows, b1, b2)
    masked = jnp.transpose(jnp.broadcast_to(mask_ref[0], (128, BK)))[:, :1]
    sides = [(pick(k_ref[...], side), pick(v_ref[...], side)) for side in range(2)]

    def body(j, carry):
        span = pl.ds(pl.multiple_of(j * BQ, BQ), BQ)
        cols = j * BQ + lax.broadcasted_iota(jnp.int32, (1, BQ), 1)
        col_seg = segment_of(cols, b1, b2)
        bias = jnp.where(row_seg == col_seg, jnp.where(rows == cols, 0.0, masked), NEG)
        queries = q_ref[span, :]
        grads = do_ref[span, :]
        place = ((j // per) ^ s_ref[3]) * per + lax.rem(j, per)
        spot = pl.ds(pl.multiple_of(place * BQ, BQ), BQ)
        out = []
        for side in range(2):
            h = 2 * pair + side
            kh, vh = sides[side]
            dk, dv = carry[2 * side], carry[2 * side + 1]
            prob = jnp.exp2(dot(kh, queries, ROW) + bias - stat_ref[h : h + 1, spot])
            score = prob * (dot(vh, grads, ROW) - stat_ref[8 + h : 9 + h, spot])
            out.append(dk + dot(score.astype(BF16), queries))
            out.append(dv + dot(prob.astype(BF16), grads))
        return tuple(out)

    zero = jnp.zeros((BK, 128), F32)
    k0, v0, k1, v1 = lax.fori_loop(j0, j1, body, (zero, zero, zero, zero))
    low = half_mask(BK, 0)
    dk_ref[...] = (jnp.where(low, k0, k1) * (1.0 / LOG2E)).astype(BF16)
    dv_ref[...] = jnp.where(low, v0, v1).astype(BF16)


def key_grads(scalars, qkv, dout, stats, kb, rows, pairs, pair):
    total = qkv.shape[0]

    def kernel(*refs):
        key_kernel(*refs, pair=pair, per=rows // BQ)

    return pl.pallas_call(
        kernel,
        grid_spec=pltpu.PrefetchScalarGridSpec(
            num_scalar_prefetch=1,
            grid=(rows // BK,),
            in_specs=[
                pl.BlockSpec((BK, 128), lambda i, s: (s[2] // BK + i, pairs + pair)),
                pl.BlockSpec((BK, 128), lambda i, s: (s[2] // BK + i, 2 * pairs + pair)),
                pl.BlockSpec((total, 128), lambda i, s: (0, pair), pipeline_mode=pl.Buffered(1)),
                pl.BlockSpec((total, 128), lambda i, s: (0, pair), pipeline_mode=pl.Buffered(1)),
                pl.BlockSpec((16, total), lambda i, s: (0, 0), pipeline_mode=pl.Buffered(1)),
                pl.BlockSpec((1, 1, BK), lambda i, s: (s[2] // BK + i, 0, 0)),
            ],
            out_specs=[
                pl.BlockSpec((BK, 128), lambda i, s: (i, 0)),
                pl.BlockSpec((BK, 128), lambda i, s: (i, 0)),
            ],
        ),
        out_shape=[jax.ShapeDtypeStruct((rows, 128), BF16)] * 2,
        compiler_params=pltpu.CompilerParams(
            dimension_semantics=("arbitrary",), vmem_limit_bytes=LIMIT
        ),
        cost_estimate=PAIR_COST,
        name="key_grads",
    )(scalars, qkv, qkv, qkv, dout, stats, kb)


def place(scalars, pieces, spots, total, cuts):
    count = len(pieces)

    def kernel(s_ref, *refs):
        ins, outs, sem = refs[:count], refs[count:-1], refs[-1]
        copies = []
        for i in range(count):
            height, start = spots[i](s_ref)
            unit = 192 if height % 192 == 0 else 16
            for k, (low, wide) in enumerate(cuts):
                copies.append(
                    pltpu.make_async_copy(
                        ins[i].at[pl.ds(0, height), pl.ds(low, wide)],
                        outs[k].at[pl.ds(pl.multiple_of(start, unit), height), :],
                        sem.at[i * len(cuts) + k],
                    )
                )
        for copy in copies:
            copy.start()
        for copy in copies:
            copy.wait()

    return pl.pallas_call(
        kernel,
        grid_spec=pltpu.PrefetchScalarGridSpec(
            num_scalar_prefetch=1,
            grid=(1,),
            in_specs=[pl.BlockSpec(memory_space=pl.ANY)] * count,
            out_specs=[pl.BlockSpec(memory_space=pl.ANY)] * len(cuts),
            scratch_shapes=[pltpu.SemaphoreType.DMA((count * len(cuts),))],
        ),
        out_shape=[jax.ShapeDtypeStruct((total, wide), BF16) for _, wide in cuts],
        name="place",
    )(scalars, *pieces)


def split(value):
    high = lax.reduce_precision(value, 8, 7)
    return high.astype(BF16), (value - high).astype(BF16)


def after(value, *others):
    return lax.optimization_barrier((value, others))[0]


def solution(mesh):
    n_fsdp, n_context = mesh.shape["fsdp"], mesh.shape["context"]
    direct_f, direct_c = n_fsdp == 4, n_context == 4
    swap = [(0, 1), (1, 0)]

    def partner(value, axis, d):
        return lax.ppermute(value, axis, [(i, i ^ d) for i in range(4)])

    def twin(value):
        return lax.ppermute(value, "tensor", swap)

    def pair_sum(value):
        low = value.astype(BF16)
        return low.astype(F32) + twin(low).astype(F32)

    def gather_weight(scalars, shard, cuts):
        if not direct_f:
            whole = lax.all_gather(shard, "fsdp", axis=0, tiled=True)
            return [whole[:, low : low + wide] for low, wide in cuts]
        rows = shard.shape[0]
        pieces = [shard] + [partner(shard, "fsdp", d) for d in (1, 2, 3)]
        spots = [lambda s, d=d: (rows, (s[6] ^ d) * rows) for d in range(4)]
        return place(scalars, pieces, spots, 4 * rows, cuts)

    def gather_rows(scalars, block, stats=None):
        if not direct_c:
            whole = lax.all_gather(block, "context", axis=0, tiled=True)
            if stats is None:
                return whole, None
            return whole, lax.all_gather(stats, "context", axis=1, tiled=True)
        core, rows = lax.axis_index("tensor"), block.shape[0]
        half = rows // 2
        mine = lax.dynamic_slice_in_dim(block, core * half, half, 0)
        if stats is not None:
            mine = jnp.concatenate((mine,) + split(stats), axis=0)
            near = partner(mine, "context", 1)
            inner = lax.ppermute(mine, "context", [(1, 2), (2, 1)])
            far = partner(mine, "context", 2)
        else:
            near = partner(mine, "context", 1)
            inner = lax.ppermute(mine, "context", [(1, 2), (2, 1)])
            far = lax.ppermute(near, "context", [(1, 2), (2, 1)]) + lax.ppermute(
                inner, "context", [(1, 0), (2, 3)]
            )
        pieces = [block]
        spots = [lambda s: (rows, s[4] * rows)]
        for d, got in ((1, near), (2, far), (3, inner)):
            pieces.append(got)
            spots.append(lambda s, d=d: (half, (s[4] ^ d) * rows + s[5] * half))
            pieces.append(twin(got))
            spots.append(lambda s, d=d: (half, (s[4] ^ d) * rows + (1 - s[5]) * half))
        whole = place(scalars, pieces, spots, 4 * rows, [(0, block.shape[1])])[0]
        if stats is None:
            return whole, None
        high = [got[half : half + 16].astype(F32) for got in (near, far, inner)]
        low = [got[half + 16 :].astype(F32) for got in (near, far, inner)]
        return whole, jnp.concatenate([stats] + [a + b for a, b in zip(high, low)], axis=1)

    def pack(small, cols):
        high, low = split(small)
        filler = jnp.zeros((16 - 2 * small.shape[0], cols), BF16)
        return jnp.concatenate([high, low, filler], axis=0)

    def unpack(block, rows):
        return block[:rows].astype(F32) + block[rows : 2 * rows].astype(F32)

    def stage_f(partial, small=None):
        if not direct_f:
            share = lax.psum_scatter(partial, "fsdp", scatter_dimension=0, tiled=True)
            return share, None if small is None else lax.psum(small, "fsdp")
        me, rows, cols = lax.axis_index("fsdp"), partial.shape[0] // 4, partial.shape[1]
        pieces = [lax.dynamic_slice_in_dim(partial, (me ^ d) * rows, rows, 0) for d in range(4)]
        if small is None:
            got = [partner(pieces[d], "fsdp", d) for d in (1, 2, 3)]
        else:
            extra = pack(small, cols)
            got = [
                partner(jnp.concatenate([pieces[d], extra], axis=0), "fsdp", d) for d in (1, 2, 3)
            ]
        parts = [pieces[0]] + [block[:rows] for block in got]
        parts = [part.astype(F32) for part in parts]
        share = ((parts[0] + parts[1]) + (parts[2] + parts[3])).astype(BF16)
        if small is None:
            return share, None
        more = [unpack(block[rows:], small.shape[0]) for block in got]
        return share, (small + more[0]) + (more[1] + more[2])

    def stage_1(share, small=None):
        if not direct_c:
            return share, small
        side, rows = lax.rem(lax.axis_index("context"), 2), share.shape[0] // 2
        mine = lax.dynamic_slice_in_dim(share, side * rows, rows, 0)
        theirs = lax.dynamic_slice_in_dim(share, (1 - side) * rows, rows, 0)
        return exchange(mine, theirs, small, 1)

    def exchange(mine, theirs, small, d):
        rows = mine.shape[0]
        if small is not None:
            theirs = jnp.concatenate([theirs, pack(small, mine.shape[1])], axis=0)
        got = partner(theirs, "context", d)
        total = (mine.astype(F32) + got[:rows].astype(F32)).astype(BF16)
        if small is not None:
            small = small + unpack(got[rows:], small.shape[0])
        return total, small

    def stage_2(share, small=None):
        if not direct_c:
            return share, small
        return exchange(share, share, small, 2)

    def stage_3(share, small=None):
        if not direct_c:
            total = lax.psum(share, "context").astype(F32)
            return total, None if small is None else lax.psum(small, "context")
        side = lax.rem(lax.axis_index("context"), 2)
        other = partner(share, "context", 1)
        first = jnp.where(side == 0, share, other)
        second = jnp.where(side == 0, other, share)
        return jnp.concatenate([first, second], axis=0).astype(F32), small

    def shards(
        tokens,
        cotangent,
        w_qkv,
        bias_qv,
        w_attn_out,
        w_up,
        bias_up,
        w_down,
        gains,
        shifts,
        seq_lengths,
        key_mask,
    ):
        rows = tokens.shape[0]
        width = w_qkv.shape[2]
        pairs = width // 128
        hidden = w_up.shape[1]
        total = key_mask.shape[0]
        dim = tokens.shape[1]
        b1 = seq_lengths[0, 0]
        b2 = b1 + seq_lengths[0, 1]
        me = lax.axis_index("context")
        order = me if direct_c else 0 * me
        scalars = jnp.stack(
            [b1, b2, me * rows, order, me, lax.axis_index("tensor"), lax.axis_index("fsdp")]
        ).astype(jnp.int32)
        kb = jnp.where(key_mask == 1, 0.0, NEG).astype(F32).reshape(total // BK, 1, BK)

        everyone, _ = gather_rows(scalars, tokens)
        shard = jnp.concatenate([w_qkv[0], w_qkv[1], w_qkv[2]], axis=1)
        (w_proj,) = gather_weight(scalars, shard, [(0, 3 * width)])
        shard = jnp.concatenate([w_attn_out.T, w_up, w_down.T], axis=1)
        shard = after(shard, w_proj)
        cuts = [(0, width), (width, hidden), (width + hidden, hidden)]
        zero = jnp.zeros((width,), F32)
        bias_row = jnp.concatenate([bias_qv[0], zero, bias_qv[1]])
        scale_row = jnp.concatenate([zero + 0.125 * LOG2E, zero + 1.0, zero + 1.0])
        qkv = ((dot(everyone, w_proj) + bias_row) * scale_row).astype(BF16)
        w_back, w_upper, w_lower = gather_weight(scalars, shard, cuts)
        attended, lse, lset = attend(scalars, qkv, kb, rows, pairs)

        branch = pair_sum(dot(attended, w_back, ROW))
        first_sum = tokens.astype(F32) + branch + shifts[0]
        normed1, factor1 = normalize(first_sum)
        first = normed1 * gains[0] + shifts[1]
        first_low = first.astype(BF16)
        upper = dot(first_low, w_upper) + bias_up
        active_f, gelu_back = jax.vjp(lambda values: jax.nn.gelu(values, approximate=False), upper)
        active = active_f.astype(BF16)
        second_sum = first + pair_sum(dot(active, w_lower, ROW)) + shifts[2]
        normed2, factor2 = normalize(second_sum)
        out = (normed2 * gains[1] + shifts[3]).astype(BF16)
        upstream = cotangent.astype(F32)
        gain_two = jnp.sum(upstream * normed2, axis=0)
        shift_three = jnp.sum(upstream, axis=0)
        grad_second = norm_back(upstream, normed2, factor2, gains[1])
        shift_two = jnp.sum(grad_second, axis=0)
        lower_grad = grad_second.astype(BF16)
        group_a, _ = stage_f(dot(lower_grad.T, active).astype(BF16))
        grad_active = dot(lower_grad, w_lower)
        grad_upper = gelu_back(grad_active)[0].astype(BF16)
        grad_bias_up = jnp.sum(grad_upper.astype(F32), axis=0)
        grad_first = grad_second + pair_sum(dot(grad_upper, w_upper, ROW))
        gain_one = jnp.sum(grad_first * normed1, axis=0)
        shift_one = jnp.sum(grad_first, axis=0)
        grad_first_sum = norm_back(grad_first, normed1, factor1, gains[0])
        shift_zero = jnp.sum(grad_first_sum, axis=0)
        branch_grad = grad_first_sum.astype(BF16)

        dout = dot(branch_grad, w_back).astype(BF16)
        marks = np.zeros((8, width), np.float32)
        for h in range(width // 64):
            marks[h, h * 64 : h * 64 + 64] = 1.0
        product = dout.astype(F32) * attended.astype(F32)
        deltat = lax.dot_general(
            jnp.asarray(marks), product, ROW, precision=lax.Precision.HIGHEST,
            preferred_element_type=F32,
        )
        branch_all, stats = gather_rows(scalars, branch_grad, jnp.concatenate([lset, deltat], axis=0))
        group_b, _ = stage_f(
            jnp.concatenate(
                [
                    dot(first_low.T, grad_upper).astype(BF16),
                    dot(branch_grad.T, attended).astype(BF16),
                ],
                axis=1,
            )
        )
        dq = query_grads(scalars, qkv, dout, attended, lse, kb, rows, pairs)
        dout_all = dot(after(branch_all, dq), w_back).astype(BF16)
        group_a, _ = stage_1(after(group_a, dq))
        group_b, _ = stage_1(after(group_b, dq))
        dk0, dv0 = key_grads(scalars, qkv, dout_all, stats, kb, rows, pairs, 0)
        dks, dvs = [dk0], [dv0]
        for pair in range(1, pairs):
            if pair == 1:
                group_a, _ = stage_2(after(group_a, dks[-1]))
                group_b, _ = stage_2(after(group_b, dks[-1]))
            elif pair == 2:
                group_a, _ = stage_3(after(group_a, dks[-1]))
                group_b, _ = stage_3(after(group_b, dks[-1]))
            dk, dv = key_grads(
                after(scalars, dks[-1]), qkv, dout_all, stats, kb, rows, pairs, pair
            )
            dks.append(dk)
            dvs.append(dv)
        if pairs < 3:
            group_a, _ = stage_3(group_a)
            group_b, _ = stage_3(group_b)
        stacked = jnp.concatenate([dq] + dks + dvs, axis=1)
        sums = jnp.sum(stacked.astype(F32), axis=0).reshape(3, width)
        small = jnp.concatenate(
            [gain_one, gain_two, shift_zero, shift_one, shift_two, shift_three, grad_bias_up, sums[0], sums[2]]
        ).reshape(-1, 3 * width)
        group_c, small = stage_f(dot(tokens.T, stacked).astype(BF16), small)
        input_part = pair_sum(dot(stacked, w_proj, ROW))
        grad_tokens = (grad_first_sum + input_part).astype(BF16)
        group_c, small = stage_1(group_c, small)
        group_c, small = stage_2(group_c, small)
        group_c, small = stage_3(group_c, small)
        small = small.reshape(-1)
        sum_gains = small[: 2 * dim].reshape(2, dim)
        sum_shifts = small[2 * dim : 6 * dim].reshape(4, dim)
        sum_bias_up = small[6 * dim : 6 * dim + hidden]
        sum_bias_qv = small[6 * dim + hidden :].reshape(2, width)
        share_qkv = jnp.stack([group_c[:, i * width : (i + 1) * width] for i in range(3)])
        share_lower = group_a.T
        share_upper = group_b[:, :hidden]
        share_back = group_b[:, hidden:].T
        return (
            out,
            grad_tokens,
            share_qkv,
            share_back,
            share_upper,
            share_lower,
            sum_bias_qv,
            sum_bias_up,
            sum_gains,
            sum_shifts,
        )

    return jax.shard_map(
        shards,
        mesh=mesh,
        in_specs=(
            P(("fsdp", "context"), None),
            P(("fsdp", "context"), None),
            P(None, "fsdp", "tensor"),
            P(None, "tensor"),
            P("tensor", "fsdp"),
            P("fsdp", "tensor"),
            P("tensor"),
            P("tensor", "fsdp"),
            P(),
            P(),
            P("fsdp", None),
            P("fsdp"),
        ),
        out_specs=(
            P(("fsdp", "context"), None),
            P(("fsdp", "context"), None),
            P(None, "fsdp", "tensor"),
            P("tensor", "fsdp"),
            P("fsdp", "tensor"),
            P("tensor", "fsdp"),
            P(None, "tensor"),
            P("tensor"),
            P(),
            P(),
        ),
        check_vma=False,
    )
```

time: 918 us -> 958 us (1.044)
  Pallas kernels: 0 us -> 638 us
  waiting for transfers between devices: 463 us -> 134 us
  matrix products: 224 us -> 57.1 us
  blocking collectives: 90.3 us -> 0 us
  starting transfers between devices: 1.29 us -> 61.2 us
  other arithmetic: 62 us -> 30.2 us
  local copies, waits for them, and re-layouts: 56.2 us -> 30.4 us
  between operations: 14.9 us -> 3.29 us
    pallas_call x0 -> x9, Pallas kernels: none -> 638 us  [the longest x4 508 us: place(): pl.pallas_call(kernel, grid_spec=pltpu.PrefetchScalarGridSpec(num_scalar_...]
    reduce_scatter x5 -> x0, waiting for transfers between devices: 198 us -> none  [the longest x1 49.3 us: shards(): lax.psum_scatter(grad_values.astype(jnp.bfloat16), 'context', scatter_dim...]
    all_gather x5 -> x0, waiting for transfers between devices: 175 us -> none  [the longest x1 45.2 us: shards(): value_piece = lax.all_gather(value_rows, 'context', axis=0, tiled=True)]
    dot_general x54 -> x14, matrix products: 224 us -> 57.1 us  [the longest x13 56 us: dot(): return lax.dot_general(a, b, dims, preferred_element_type=F32)]
    ppermute x0 -> x41, waiting for transfers between devices: none -> 134 us  [the longest x27 119 us: partner(): return lax.ppermute(value, axis, [(i, i ^ d) for i in range(4)])]
    psum x1 -> x0, blocking collectives: 79.4 us -> none  [shards(): lax.psum((grad_bias_qv, grad_bias_up, gain_rows, shift_rows), ('fsdp', 'c...]
    psum x5 -> x0, waiting for transfers between devices: 77.3 us -> none  [the longest x1 21.2 us: shards(): lax.psum(part_qkv.astype(jnp.bfloat16), 'context').astype(jnp.float32)]
    ppermute x0 -> x41, starting transfers between devices: none -> 61.2 us  [the longest x27 56.2 us: partner(): return lax.ppermute(value, axis, [(i, i ^ d) for i in range(4)])]
  transfers between devices with their start and end apart: 16 -> 41, of which waited for: 15 -> 15; matrix products, arithmetic and copies ran while one was open for 8% -> 5% of each run, Pallas kernels for 0% -> 30%
where the time goes in v1:
time: 958 us; the launch traced here: 954 us
  Pallas kernels  638 us (67%)
  waiting for transfers between devices  134 us (14%)
  starting transfers between devices  61.2 us (6%)
  matrix products  57.1 us (6%)
  local copies, waits for them, and re-layouts  30.4 us (3%)
  other arithmetic  30.2 us (3%)
    pallas_call x4, Pallas kernels, place(): pl.pallas_call(kernel, grid_spec=pltpu.PrefetchScalarGridSpec(num_scalar_...  508 us
    ppermute x27, waiting for transfers between devices, partner(): return lax.ppermute(value, axis, [(i, i ^ d) for i in range(4)])  119 us
    ppermute x27, starting transfers between devices, partner(): return lax.ppermute(value, axis, [(i, i ^ d) for i in range(4)])  56.2 us
    dot_general x13, matrix products, dot(): return lax.dot_general(a, b, dims, preferred_element_type=F32)  56 us
    pallas_call x1, Pallas kernels, query_grads(): pl.pallas_call(query_kernel, grid_spec=pltpu.PrefetchScalarGridSpec(num_s...  47.1 us
    pallas_call x3, Pallas kernels, key_grads(): pl.pallas_call(kernel, grid_spec=pltpu.PrefetchScalarGridSpec(num_scalar_...  45 us
    pallas_call x1, Pallas kernels, attend(): pl.pallas_call(attend_kernel, grid_spec=pltpu.PrefetchScalarGridSpec(num_...  38 us
  transfers between devices with their start and end apart: 41, of which 15 were waited for; matrix products, arithmetic and copies ran while one was open for 5% of the time, Pallas kernels for 30%

profile of v1, /device:TPU:0, one launch (start us, length us, event | category | flops | bytes accessed | tf_op | source)
XLA Modules:
  0.0 954.3 jit_solution(15160964843493202519)
XLA Ops:
  1.8 3.1 collective-permute-start
  6.7 11.5 %collective-permute-done.refs_1_ = bf16[384,768]{1,0:T(8,128)(2,1)S(1)} collective-permute-done((bf16[384,768]{1,0:T(8,128)(2,1)S(1)}, bf16[384,768]{1,0:T(8,128)(2,1)S(1)}, u32[]{:S(2)}, u32[]{:S(2)}) %collective-permute-start) | collective-permute-done | bytes 589856 | tf_op jit(solution)/shard_map/ppermute | solution.py:353
  19.0 1.3 collective-permute-start.4
  20.3 1.7 collective-permute-start.7
  22.0 1.5 collective-permute-start.8
  27.8 9.1 collective-permute-done.4
  37.2 2.5 collective-permute-start.9
  39.7 1.4 pad_maximum_fusion.refs_0_
  41.1 9.7 %collective-permute-done.9.refs_3_ = bf16[192,1152]{1,0:T(8,128)(2,1)} collective-permute-done((bf16[192,1152]{1,0:T(8,128)(2,1)S(1)}, bf16[192,1152]{1,0:T(8,128)(2,1)}, u32[]{:S(2)}, u32[]{:S(2)}) %collective-permute-start.9) | collective-permute-done | bytes 442400 | tf_op jit(solution)/shard_map/ppermute | solution.py:353
  50.9 55.4 %place.5 = bf16[768,1152]{1,0:T(8,128)(2,1)} custom-call(s32[7]{0:T(128)} %stack.36.s_ref.refs_0_, bf16[192,1152]{1,0:T(8,128)(2,1)} %copy-done.14, bf16[192,1152]{1,0:T(8,128)(2,1)} %collective-permute-done.7.refs_1_, bf16[192,1152]{1,0:T(8,128)(2,1)} %collective-permute-done.8.refs_2_, bf16[192,1152]{1,0:T(8,128)(2,1)} %collective-permute-done.9.refs_3_), custom_call_target="tpu_custom_call" | custom-call | tf_op jit(solution)/shard_map/place/pallas_call | solution.py:324
  106.3 1.6 collective-permute-start.10
  107.8 1.5 collective-permute-start.11
  109.9 144.9 %place.4 = bf16[3072,768]{1,0:T(8,128)(2,1)} custom-call(s32[7]{0:T(128)} %stack.36.s_ref.refs_0_, bf16[768,768]{1,0:T(8,128)(2,1)} %refs_0_.1, bf16[384,768]{1,0:T(8,128)(2,1)} %copy-done.21, bf16[384,768]{1,0:T(8,128)(2,1)} %collective-permute-done.1.refs_2_, bf16[384,768]{1,0:T(8,128)(2,1)} %copy-done.9, bf16[384,768]{1,0:T(8,128)(2,1)} %collective-permute-done.5.refs_4_, ...), custom_call_target="tpu_custom_call" | custom-call | tf_op jit(solution)/shard_map/place/pallas_call | solution.py:324
  254.8 11.8 %multiply_convert_fusion.q_ref.k_ref.v_ref.refs_1_.refs_2_.refs_3_ = bf16[3072,1152]{1,0:T(8,128)(2,1)} fusion(bf16[3072,768]{1,0:T(8,128)(2,1)} %place.4, bf16[768,1152]{1,0:T(8,128)(2,1)S(1)} %copy-done.12, f32[1152]{0:T(1024)S(1)} %copy-done.49, f32[1152]{0:T(1024)S(1)} %pad_maximum_fusion.18), kind=kOutput, calls=%fused_computation | convolution fusion | flops 5446434816 | bytes 13575168 | tf_op jit(solution)/shard_map/dot_general | solution.py:24
  266.6 38.0 %attend.1 = (bf16[768,384]{1,0:T(8,128)(2,1)}, f32[768,128]{1,0:T(8,128)}, f32[8,768]{1,0:T(8,128)}) custom-call(s32[7]{0:T(128)} %stack.36.s_ref.refs_0_, bf16[3072,1152]{1,0:T(8,128)(2,1)} %multiply_convert_fusion.q_ref.k_ref.v_ref.refs_1_.refs_2_.refs_3_, bf16[3072,1152]{1,0:T(8,128)(2,1)} %multiply_convert_fusion.q_ref.k_ref.v_ref.refs_1_.refs_2_.refs_3_, ...), custom_call_target="tpu_custom_call" | custom-call | flops 35999997952 | bytes 8000000 | tf_op jit(solution)/shard_map/attend/pallas_call | solution.py:127
  304.6 162.8 %place.6 = (bf16[768,384]{1,0:T(8,128)(2,1)}, bf16[768,1536]{1,0:T(8,128)(2,1)}, bf16[768,1536]{1,0:T(8,128)(2,1)}) custom-call(s32[7]{0:T(128)} %stack.36.s_ref.refs_0_, bf16[192,3456]{1,0:T(8,128)(2,1)} %copy-done.7, bf16[192,3456]{1,0:T(8,128)(2,1)} %collective-permute-done.10.refs_1_, bf16[192,3456]{1,0:T(8,128)(2,1)} %collective-permute-done.11.refs_2_, ...), custom_call_target="tpu_custom_call" | custom-call | tf_op jit(solution)/shard_map/place/pallas_call | solution.py:324
  467.5 1.9 convolution_convert_fusion.5
  469.6 2.7 collective-permute-done.13
  474.6 13.5 %multiply_convert_fusion.1 = (bf16[768,1536]{1,0:T(8,128)(2,1)S(1)}, f32[768,1536]{1,0:T(8,128)}, f32[768,1536]{1,0:T(8,128)}) fusion(f32[1536]{0:T(1024)S(1)} %copy-done.48, bf16[768,1536]{1,0:T(8,128)(2,1)S(1)} %copy-done.44, f32[768,768]{1,0:T(8,128)S(1)} %get-tuple-element.82, f32[768]{0:T(1024)S(1)} %get-tuple-element.63, ...), kind=kOutput, calls=%fused_computation.9 | convolution fusion | flops 1892745216 | bytes 16533504 | tf_op jit(solution)/shard_map/dot_general | solution.py:24
  488.2 3.0 convolution_convert_fusion.7
  491.4 3.0 collective-permute-done.14
  494.4 2.6 fusion.40
  498.3 1.7 fusion.12
  500.0 2.8 fusion.37
  502.8 2.0 convolution_convert_fusion.1
  507.2 4.0 convert_reduce_fusion
  511.3 3.0 convolution_convert_fusion.6
  514.5 1.3 constant_dynamic-slice_fusion.3
  515.8 8.1 collective-permute-start.36
  523.9 4.0 convolution_convert_fusion.2
  527.9 4.3 collective-permute-done.35
  532.2 18.2 %collective-permute-done.36 = bf16[192,1536]{1,0:T(8,128)(2,1)} collective-permute-done((bf16[192,1536]{1,0:T(8,128)(2,1)}, bf16[192,1536]{1,0:T(8,128)(2,1)}, u32[]{:S(2)}, u32[]{:S(2)}) %collective-permute-start.36) | collective-permute-done | bytes 589856 | tf_op jit(solution)/shard_map/ppermute | solution.py:353
  550.4 1.9 add_convert_fusion.4
  552.3 2.9 multiply_reduce_fusion
  556.3 1.4 copy-done.25
  560.5 5.3 collective-permute-start.18
  566.6 47.1 %query_grads.1 = bf16[768,384]{1,0:T(8,128)(2,1)} custom-call(s32[7]{0:T(128)} %stack.36.s_ref.refs_0_, bf16[3072,1152]{1,0:T(8,128)(2,1)} %multiply_convert_fusion.q_ref.k_ref.v_ref.refs_1_.refs_2_.refs_3_, bf16[3072,1152]{1,0:T(8,128)(2,1)} %multiply_convert_fusion.q_ref.k_ref.v_ref.refs_1_.refs_2_.refs_3_, ...), custom_call_target="tpu_custom_call" | custom-call | flops 35999997952 | bytes 8000000 | tf_op jit(solution)/shard_map/query_grads/pallas_call | solution.py:205
  613.8 2.1 collective-permute-start.38
  616.1 7.2 collective-permute-start.30
  624.6 1.3 constant_dynamic-update-slice_fusion.8
  627.2 1.3 constant_dynamic-update-slice_fusion.14
  628.5 1.3 constant_dynamic-update-slice_fusion.13
  629.8 1.3 constant_dynamic-update-slice_fusion.12
  631.1 1.3 constant_dynamic-update-slice_fusion.11
  635.5 18.6 %collective-permute-done.30 = bf16[192,1920]{1,0:T(8,128)(2,1)S(1)} collective-permute-done((bf16[192,1920]{1,0:T(8,128)(2,1)S(1)}, bf16[192,1920]{1,0:T(8,128)(2,1)S(1)}, u32[]{:S(2)}, u32[]{:S(2)}) %collective-permute-start.30) | collective-permute-done | bytes 737312 | tf_op jit(solution)/shard_map/ppermute | solution.py:353
  655.8 7.1 collective-permute-done.32
  664.7 144.8 %place.7 = bf16[3072,768]{1,0:T(8,128)(2,1)} custom-call(s32[7]{0:T(128)} %stack.36.s_ref.refs_0_, bf16[768,768]{1,0:T(8,128)(2,1)} %copy-done.4, bf16[416,768]{1,0:T(8,128)(2,1)} %collective-permute-done.16.refs_1_, bf16[416,768]{1,0:T(8,128)(2,1)} %copy-done.19, bf16[416,768]{1,0:T(8,128)(2,1)} %copy-done.17, bf16[416,768]{1,0:T(8,128)(2,1)} %copy-done.20, ...), custom_call_target="tpu_custom_call" | custom-call | tf_op jit(solution)/shard_map/place/pallas_call | solution.py:324
  809.5 6.5 convolution_convert_fusion.refs_4_
  816.0 15.0 %key_grads.3 = (bf16[768,128]{1,0:T(8,128)(2,1)}, bf16[768,128]{1,0:T(8,128)(2,1)}) custom-call(s32[7]{0:T(128)} %stack.36.s_ref.refs_0_, bf16[3072,1152]{1,0:T(8,128)(2,1)} %multiply_convert_fusion.q_ref.k_ref.v_ref.refs_1_.refs_2_.refs_3_, bf16[3072,1152]{1,0:T(8,128)(2,1)} %multiply_convert_fusion.q_ref.k_ref.v_ref.refs_1_.refs_2_.refs_3_, ...), custom_call_target="tpu_custom_call" | custom-call | flops 14000000000 | bytes 4000000 | tf_op jit(solution)/shard_map/key_grads/pallas_call | solution.py:275
  831.0 14.9 %key_grads.4 = (bf16[768,128]{1,0:T(8,128)(2,1)}, bf16[768,128]{1,0:T(8,128)(2,1)}) custom-call(s32[7]{0:T(128)} %stack.36.s_ref.refs_0_, bf16[3072,1152]{1,0:T(8,128)(2,1)} %multiply_convert_fusion.q_ref.k_ref.v_ref.refs_1_.refs_2_.refs_3_, bf16[3072,1152]{1,0:T(8,128)(2,1)} %multiply_convert_fusion.q_ref.k_ref.v_ref.refs_1_.refs_2_.refs_3_, ...), custom_call_target="tpu_custom_call" | custom-call | flops 14000000000 | bytes 4000000 | tf_op jit(solution)/shard_map/key_grads/pallas_call | solution.py:275
  846.0 15.1 %key_grads.5 = (bf16[768,128]{1,0:T(8,128)(2,1)}, bf16[768,128]{1,0:T(8,128)(2,1)}) custom-call(s32[7]{0:T(128)} %stack.36.s_ref.refs_0_, bf16[3072,1152]{1,0:T(8,128)(2,1)} %multiply_convert_fusion.q_ref.k_ref.v_ref.refs_1_.refs_2_.refs_3_, bf16[3072,1152]{1,0:T(8,128)(2,1)} %multiply_convert_fusion.q_ref.k_ref.v_ref.refs_1_.refs_2_.refs_3_, ...), custom_call_target="tpu_custom_call" | custom-call | flops 14000000000 | bytes 4000000 | tf_op jit(solution)/shard_map/key_grads/pallas_call | solution.py:275
  863.6 1.8 convolution_convert_fusion.3
  868.0 1.4 reshape.88
  870.5 7.6 collective-permute-start.24
  878.1 10.6 %collective-permute-start.39 = (bf16[96,1536]{1,0:T(8,128)(2,1)S(1)}, bf16[96,1536]{1,0:T(8,128)(2,1)S(1)}, u32[]{:S(2)}, u32[]{:S(2)}) collective-permute-start(bf16[96,1536]{1,0:T(8,128)(2,1)S(1)} %copy-done.16), channel_id=1, source_target_pairs={{0,4},{2,6},{4,0},{6,2},{1,5},{3,7},{5,1},{7,3},{8,12},{10,14},{12... | collective-permute-start | bytes 884744 | tf_op jit(solution)/shard_map/ppermute | solution.py:353
  888.7 2.8 convolution_convert_fusion.4
  891.5 7.4 collective-permute-done.39
  899.0 7.7 collective-permute-done.33
  906.8 2.1 collective-permute-start.34
  909.4 7.2 collective-permute-done.40
  917.8 11.3 %collective-permute-done.26 = bf16[112,1152]{1,0:T(8,128)(2,1)S(1)} collective-permute-done((bf16[112,1152]{1,0:T(8,128)(2,1)S(1)}, bf16[112,1152]{1,0:T(8,128)(2,1)S(1)}, u32[]{:S(2)}, u32[]{:S(2)}) %collective-permute-start.26) | collective-permute-done | bytes 258080 | tf_op jit(solution)/shard_map/ppermute | solution.py:353
  931.3 11.7 %collective-permute-done.27 = bf16[112,1152]{1,0:T(8,128)(2,1)S(1)} collective-permute-done((bf16[112,1152]{1,0:T(8,128)(2,1)S(1)}, bf16[112,1152]{1,0:T(8,128)(2,1)S(1)}, u32[]{:S(2)}, u32[]{:S(2)}) %collective-permute-start.27) | collective-permute-done | bytes 258080 | tf_op jit(solution)/shard_map/ppermute | solution.py:353
  945.6 3.0 add_convert_fusion.1
  948.6 4.3 collective-permute-done.28
  (253 shorter events, 41.6 us)
Async XLA Ops:
  0.6 22.9 %copy-start.43 = (s32[1,3]{1,0:T(1,128)S(1)}, s32[1,3]{1,0:T(1,128)}, u32[]{:S(2)}) copy-start(s32[1,3]{1,0:T(1,128)} %param.23) | copy-start | bytes 40
  0.7 26.0 %copy-start.42 = (f32[2,384]{1,0:T(2,128)S(1)}, f32[2,384]{1,0:T(2,128)}, u32[]{:S(2)}) copy-start(f32[2,384]{1,0:T(2,128)} %param.16) | copy-start | bytes 9220
  0.7 26.0 %copy-start.39 = (s32[3072]{0:T(1024)S(1)}, s32[3072]{0:T(1024)}, u32[]{:S(2)}) copy-start(s32[3072]{0:T(1024)} %param.24) | copy-start | bytes 36868
  1.8 16.4 %collective-permute-start = (bf16[384,768]{1,0:T(8,128)(2,1)S(1)}, bf16[384,768]{1,0:T(8,128)(2,1)S(1)}, u32[]{:S(2)}, u32[]{:S(2)}) collective-permute-start(bf16[384,768]{1,0:T(8,128)(2,1)S(1)} %constant_dynamic-slice_fusion.7), channel_id=1, source_target_pairs={{0,2},{2,0},{4,6},{6,4},{1,3},{3,1},{5,7},{7,5},{8,10},{10,8},{12,... | collective-permute-start | bytes 1769480 | tf_op jit(solution)/shard_map/ppermute | solution.py:353
  4.9 14.0 %collective-permute-start.3 = (bf16[384,768]{1,0:T(8,128)(2,1)S(1)}, bf16[384,768]{1,0:T(8,128)(2,1)S(1)}, u32[]{:S(2)}, u32[]{:S(2)}) collective-permute-start(bf16[384,768]{1,0:T(8,128)(2,1)S(1)} %constant_dynamic-slice_fusion.7), channel_id=1, source_target_pairs={{2,4},{4,2},{3,5},{5,3},{10,12},{12,10},{11,13},{13,11},{18,20},{2... | collective-permute-start | bytes 1769480 | tf_op jit(solution)/shard_map/ppermute | solution.py:387
  18.2 22.9 %copy-start.21 = (bf16[384,768]{1,0:T(8,128)(2,1)}, bf16[384,768]{1,0:T(8,128)(2,1)S(1)}, u32[]{:S(2)}) copy-start(bf16[384,768]{1,0:T(8,128)(2,1)S(1)} %collective-permute-done.refs_1_) | copy-start | bytes 1769476
  18.2 9.1 collective-permute-start.2
  18.9 22.2 %copy-start.22 = (bf16[384,768]{1,0:T(8,128)(2,1)}, bf16[384,768]{1,0:T(8,128)(2,1)S(1)}, u32[]{:S(2)}) copy-start(bf16[384,768]{1,0:T(8,128)(2,1)S(1)} %collective-permute-done.3.refs_5_) | copy-start | bytes 1769476
  19.0 18.0 %collective-permute-start.4 = (bf16[384,768]{1,0:T(8,128)(2,1)S(1)}, bf16[384,768]{1,0:T(8,128)(2,1)S(1)}, u32[]{:S(2)}, u32[]{:S(2)}) collective-permute-start(bf16[384,768]{1,0:T(8,128)(2,1)S(1)} %collective-permute-done.3.refs_5_), channel_id=1, source_target_pairs={{2,0},{4,6},{3,1},{5,7},{10,8},{12,14},{11,9},{13,15},{18,16},{20,... | collective-permute-start | bytes 1769480 | tf_op jit(solution)/shard_map/ppermute | solution.py:388
  20.3 30.5 %copy-start.14 = (bf16[192,1152]{1,0:T(8,128)(2,1)}, bf16[192,1152]{1,0:T(8,128)(2,1)S(1)}, u32[]{:S(2)}) copy-start(bf16[192,1152]{1,0:T(8,128)(2,1)S(1)} %pad_maximum_fusion.13.refs_0_) | copy-start | bytes 1327108
  20.3 16.9 %collective-permute-start.7 = (bf16[192,1152]{1,0:T(8,128)(2,1)S(1)}, bf16[192,1152]{1,0:T(8,128)(2,1)}, u32[]{:S(2)}, u32[]{:S(2)}) collective-permute-start(bf16[192,1152]{1,0:T(8,128)(2,1)S(1)} %pad_maximum_fusion.13.refs_0_), channel_id=1, source_target_pairs={{0,8},{8,0},{16,24},{24,16},{1,9},{9,1},{17,25},{25,17},{2,10},{10... | collective-permute-start | bytes 1327112 | tf_op jit(solution)/shard_map/ppermute | solution.py:353
  22.0 19.1 %collective-permute-start.8 = (bf16[192,1152]{1,0:T(8,128)(2,1)S(1)}, bf16[192,1152]{1,0:T(8,128)(2,1)}, u32[]{:S(2)}, u32[]{:S(2)}) collective-permute-start(bf16[192,1152]{1,0:T(8,128)(2,1)S(1)} %pad_maximum_fusion.13.refs_0_), channel_id=1, source_target_pairs={{0,16},{8,24},{16,0},{24,8},{1,17},{9,25},{17,1},{25,9},{2,18},{10... | collective-permute-start | bytes 1327112 | tf_op jit(solution)/shard_map/ppermute | solution.py:353
  27.3 82.0 %collective-permute-start.1 = (bf16[384,768]{1,0:T(8,128)(2,1)S(1)}, bf16[384,768]{1,0:T(8,128)(2,1)}, u32[]{:S(2)}, u32[]{:S(2)}) collective-permute-start(bf16[384,768]{1,0:T(8,128)(2,1)S(1)} %collective-permute-done.refs_1_), channel_id=1, source_target_pairs={{0,1},{1,0},{2,3},{3,2},{4,5},{5,4},{6,7},{7,6},{8,9},{9,8},{10,11... | collective-permute-start | bytes 1769480 | tf_op jit(solution)/shard_map/ppermute | solution.py:356
  27.3 82.5 %collective-permute-start.6 = (bf16[384,768]{1,0:T(8,128)(2,1)S(1)}, bf16[384,768]{1,0:T(8,128)(2,1)}, u32[]{:S(2)}, u32[]{:S(2)}) collective-permute-start(bf16[384,768]{1,0:T(8,128)(2,1)S(1)} %collective-permute-done.3.refs_5_), channel_id=1, source_target_pairs={{0,1},{1,0},{2,3},{3,2},{4,5},{5,4},{6,7},{7,6},{8,9},{9,8},{10,11... | collective-permute-start | bytes 1769480 | tf_op jit(solution)/shard_map/ppermute | solution.py:356
  37.1 69.2 %copy-start.9 = (bf16[384,768]{1,0:T(8,128)(2,1)}, bf16[384,768]{1,0:T(8,128)(2,1)S(1)}, u32[]{:S(2)}) copy-start(bf16[384,768]{1,0:T(8,128)(2,1)S(1)} %add.223.refs_3_) | copy-start | bytes 1769476
  37.1 72.7 %collective-permute-start.5 = (bf16[384,768]{1,0:T(8,128)(2,1)S(1)}, bf16[384,768]{1,0:T(8,128)(2,1)}, u32[]{:S(2)}, u32[]{:S(2)}) collective-permute-start(bf16[384,768]{1,0:T(8,128)(2,1)S(1)} %add.223.refs_3_), channel_id=1, source_target_pairs={{0,1},{1,0},{2,3},{3,2},{4,5},{5,4},{6,7},{7,6},{8,9},{9,8},{10,11... | collective-permute-start | bytes 1769480 | tf_op jit(solution)/shard_map/ppermute | solution.py:356
  37.2 13.6 %collective-permute-start.9 = (bf16[192,1152]{1,0:T(8,128)(2,1)S(1)}, bf16[192,1152]{1,0:T(8,128)(2,1)}, u32[]{:S(2)}, u32[]{:S(2)}) collective-permute-start(bf16[192,1152]{1,0:T(8,128)(2,1)S(1)} %pad_maximum_fusion.13.refs_0_), channel_id=1, source_target_pairs={{0,24},{8,16},{16,8},{24,0},{1,25},{9,17},{17,9},{25,1},{2,26},{10... | collective-permute-start | bytes 1327112 | tf_op jit(solution)/shard_map/ppermute | solution.py:353
  41.1 213.6 %copy-start.7 = (bf16[192,3456]{1,0:T(8,128)(2,1)}, bf16[192,3456]{1,0:T(8,128)(2,1)S(1)}, u32[]{:S(2)}) copy-start(bf16[192,3456]{1,0:T(8,128)(2,1)S(1)} %pad_maximum_fusion.refs_0_) | copy-start | bytes 3981316
  106.3 148.5 %copy-start.49 = (f32[1152]{0:T(1024)S(1)}, f32[1152]{0:T(1024)}, u32[]{:S(2)}) copy-start(f32[1152]{0:T(1024)} %constant.18.clone.1) | copy-start | bytes 13828
  106.3 198.3 %collective-permute-start.10 = (bf16[192,3456]{1,0:T(8,128)(2,1)S(1)}, bf16[192,3456]{1,0:T(8,128)(2,1)}, u32[]{:S(2)}, u32[]{:S(2)}) collective-permute-start(bf16[192,3456]{1,0:T(8,128)(2,1)S(1)} %pad_maximum_fusion.refs_0_), channel_id=1, source_target_pairs={{0,8},{8,0},{16,24},{24,16},{1,9},{9,1},{17,25},{25,17},{2,10},{10... | collective-permute-start | bytes 3981320 | tf_op jit(solution)/shard_map/ppermute | solution.py:353
  107.8 196.8 %collective-permute-start.11 = (bf16[192,3456]{1,0:T(8,128)(2,1)S(1)}, bf16[192,3456]{1,0:T(8,128)(2,1)}, u32[]{:S(2)}, u32[]{:S(2)}) collective-permute-start(bf16[192,3456]{1,0:T(8,128)(2,1)S(1)} %pad_maximum_fusion.refs_0_), channel_id=1, source_target_pairs={{0,16},{8,24},{16,0},{24,8},{1,17},{9,25},{17,1},{25,9},{2,18},{10... | collective-permute-start | bytes 3981320 | tf_op jit(solution)/shard_map/ppermute | solution.py:353
  109.4 195.3 %collective-permute-start.12 = (bf16[192,3456]{1,0:T(8,128)(2,1)S(1)}, bf16[192,3456]{1,0:T(8,128)(2,1)}, u32[]{:S(2)}, u32[]{:S(2)}) collective-permute-start(bf16[192,3456]{1,0:T(8,128)(2,1)S(1)} %pad_maximum_fusion.refs_0_), channel_id=1, source_target_pairs={{0,24},{8,16},{16,8},{24,0},{1,25},{9,17},{17,9},{25,1},{2,26},{10... | collective-permute-start | bytes 3981320 | tf_op jit(solution)/shard_map/ppermute | solution.py:353
  109.8 144.9 %copy-start.12 = (bf16[768,1152]{1,0:T(8,128)(2,1)S(1)}, bf16[768,1152]{1,0:T(8,128)(2,1)}, u32[]{:S(2)}) copy-start(bf16[768,1152]{1,0:T(8,128)(2,1)} %place.5) | copy-start | bytes 5308420
  304.6 162.9 %copy-start.11 = (bf16[768,384]{1,0:T(8,128)(2,1)S(1)}, bf16[768,384]{1,0:T(8,128)(2,1)}, u32[]{:S(2)}) copy-start(bf16[768,384]{1,0:T(8,128)(2,1)} %get-tuple-element.32.o_ref) | copy-start | bytes 1769476
  469.5 2.9 collective-permute-start.13
  491.2 3.2 collective-permute-start.14
  514.3 38.0 %collective-permute-start.15 = (bf16[768,768]{1,0:T(8,128)(2,1)}, bf16[768,768]{1,0:T(8,128)(2,1)}, u32[]{:S(2)}, u32[]{:S(2)}) collective-permute-start(bf16[768,768]{1,0:T(8,128)(2,1)} %convolution_convert_fusion.6), channel_id=1, source_target_pairs={{0,1},{1,0},{2,3},{3,2},{4,5},{5,4},{6,7},{7,6},{8,9},{9,8},{10,11... | collective-permute-start | bytes 3538952 | tf_op jit(solution)/shard_map/ppermute | solution.py:356
  515.8 16.4 %collective-permute-start.35 = (bf16[192,1536]{1,0:T(8,128)(2,1)}, bf16[192,1536]{1,0:T(8,128)(2,1)S(1)}, u32[]{:S(2)}, u32[]{:S(2)}) collective-permute-start(bf16[192,1536]{1,0:T(8,128)(2,1)} %get-tuple-element.87), channel_id=1, source_target_pairs={{0,8},{8,0},{16,24},{24,16},{1,9},{9,1},{17,25},{25,17},{2,10},{10... | collective-permute-start | bytes 1769480 | tf_op jit(solution)/shard_map/ppermute | solution.py:353
  515.8 34.6 %collective-permute-start.36 = (bf16[192,1536]{1,0:T(8,128)(2,1)}, bf16[192,1536]{1,0:T(8,128)(2,1)}, u32[]{:S(2)}, u32[]{:S(2)}) collective-permute-start(bf16[192,1536]{1,0:T(8,128)(2,1)} %get-tuple-element.89), channel_id=1, source_target_pairs={{0,16},{8,24},{16,0},{24,8},{1,17},{9,25},{17,1},{25,9},{2,18},{10... | collective-permute-start | bytes 1769480 | tf_op jit(solution)/shard_map/ppermute | solution.py:353
  523.9 26.5 %collective-permute-start.37 = (bf16[192,1536]{1,0:T(8,128)(2,1)}, bf16[192,1536]{1,0:T(8,128)(2,1)}, u32[]{:S(2)}, u32[]{:S(2)}) collective-permute-start(bf16[192,1536]{1,0:T(8,128)(2,1)} %get-tuple-element.88), channel_id=1, source_target_pairs={{0,24},{8,16},{16,8},{24,0},{1,25},{9,17},{17,9},{25,1},{2,26},{10... | collective-permute-start | bytes 1769480 | tf_op jit(solution)/shard_map/ppermute | solution.py:353
  527.9 24.4 %copy-start.3 = (f32[768,768]{1,0:T(8,128)S(1)}, f32[768,768]{1,0:T(8,128)}, u32[]{:S(2)}) copy-start(f32[768,768]{1,0:T(8,128)} %copy-done.2) | copy-start | bytes 7077892
  532.2 18.2 %copy-start.26 = (bf16[192,1536]{1,0:T(8,128)(2,1)}, bf16[192,1536]{1,0:T(8,128)(2,1)S(1)}, u32[]{:S(2)}) copy-start(bf16[192,1536]{1,0:T(8,128)(2,1)S(1)} %collective-permute-done.35) | copy-start | bytes 1769476
  560.5 74.2 %collective-permute-start.18 = (bf16[416,768]{1,0:T(8,128)(2,1)}, bf16[416,768]{1,0:T(8,128)(2,1)S(1)}, u32[]{:S(2)}, u32[]{:S(2)}) collective-permute-start(bf16[416,768]{1,0:T(8,128)(2,1)} %pad_maximum_fusion.11), channel_id=1, source_target_pairs={{0,4},{2,6},{4,0},{6,2},{1,5},{3,7},{5,1},{7,3},{8,12},{10,14},{12... | collective-permute-start | bytes 1916936 | tf_op jit(solution)/shard_map/ppermute | solution.py:353
  565.8 67.5 %collective-permute-start.16 = (bf16[416,768]{1,0:T(8,128)(2,1)}, bf16[416,768]{1,0:T(8,128)(2,1)}, u32[]{:S(2)}, u32[]{:S(2)}) collective-permute-start(bf16[416,768]{1,0:T(8,128)(2,1)} %pad_maximum_fusion.11), channel_id=1, source_target_pairs={{0,2},{2,0},{4,6},{6,4},{1,3},{3,1},{5,7},{7,5},{8,10},{10,8},{12,... | collective-permute-start | bytes 1916936 | tf_op jit(solution)/shard_map/ppermute | solution.py:353
  613.8 17.3 %copy-start.40 = (f32[1536]{0:T(1024)S(1)}, f32[1536]{0:T(1024)}, u32[]{:S(2)}) copy-start(f32[1536]{0:T(1024)} %get-tuple-element.117) | copy-start | bytes 18436
  613.8 18.6 %copy-start.23 = (bf16[768,384]{1,0:T(8,128)(2,1)S(1)}, bf16[768,384]{1,0:T(8,128)(2,1)}, u32[]{:S(2)}) copy-start(bf16[768,384]{1,0:T(8,128)(2,1)} %query_grads.1) | copy-start | bytes 1769476
  613.8 18.6 %collective-permute-start.38 = (bf16[96,1536]{1,0:T(8,128)(2,1)S(1)}, bf16[96,1536]{1,0:T(8,128)(2,1)S(1)}, u32[]{:S(2)}, u32[]{:S(2)}) collective-permute-start(bf16[96,1536]{1,0:T(8,128)(2,1)S(1)} %constant_dynamic-slice_fusion), channel_id=1, source_target_pairs={{0,2},{2,0},{4,6},{6,4},{1,3},{3,1},{5,7},{7,5},{8,10},{10,8},{12,... | collective-permute-start | bytes 884744 | tf_op jit(solution)/shard_map/ppermute | solution.py:353
  616.0 18.9 %collective-permute-start.29 = (bf16[192,1920]{1,0:T(8,128)(2,1)S(1)}, bf16[192,1920]{1,0:T(8,128)(2,1)S(1)}, u32[]{:S(2)}, u32[]{:S(2)}) collective-permute-start(bf16[192,1920]{1,0:T(8,128)(2,1)S(1)} %get-tuple-element.83), channel_id=1, source_target_pairs={{0,8},{8,0},{16,24},{24,16},{1,9},{9,1},{17,25},{25,17},{2,10},{10... | collective-permute-start | bytes 2211848 | tf_op jit(solution)/shard_map/ppermute | solution.py:353
  616.1 38.0 %collective-permute-start.30 = (bf16[192,1920]{1,0:T(8,128)(2,1)S(1)}, bf16[192,1920]{1,0:T(8,128)(2,1)S(1)}, u32[]{:S(2)}, u32[]{:S(2)}) collective-permute-start(bf16[192,1920]{1,0:T(8,128)(2,1)S(1)} %get-tuple-element.84), channel_id=1, source_target_pairs={{0,16},{8,24},{16,0},{24,8},{1,17},{9,25},{17,1},{25,9},{2,18},{10... | collective-permute-start | bytes 2211848 | tf_op jit(solution)/shard_map/ppermute | solution.py:353
  632.4 21.7 %collective-permute-start.31 = (bf16[192,1920]{1,0:T(8,128)(2,1)S(1)}, bf16[192,1920]{1,0:T(8,128)(2,1)S(1)}, u32[]{:S(2)}, u32[]{:S(2)}) collective-permute-start(bf16[192,1920]{1,0:T(8,128)(2,1)S(1)} %get-tuple-element.85), channel_id=1, source_target_pairs={{0,24},{8,16},{16,8},{24,0},{1,25},{9,17},{17,9},{25,1},{2,26},{10... | collective-permute-start | bytes 2211848 | tf_op jit(solution)/shard_map/ppermute | solution.py:353
  633.3 21.6 %collective-permute-start.20 = (bf16[416,768]{1,0:T(8,128)(2,1)}, bf16[416,768]{1,0:T(8,128)(2,1)S(1)}, u32[]{:S(2)}, u32[]{:S(2)}) collective-permute-start(bf16[416,768]{1,0:T(8,128)(2,1)} %pad_maximum_fusion.11), channel_id=1, source_target_pairs={{2,4},{4,2},{3,5},{5,3},{10,12},{12,10},{11,13},{13,11},{18,20},{2... | collective-permute-start | bytes 1916936 | tf_op jit(solution)/shard_map/ppermute | solution.py:383
  634.8 19.7 %copy-start.17 = (bf16[416,768]{1,0:T(8,128)(2,1)}, bf16[416,768]{1,0:T(8,128)(2,1)S(1)}, u32[]{:S(2)}) copy-start(bf16[416,768]{1,0:T(8,128)(2,1)S(1)} %collective-permute-done.18.refs_3_) | copy-start | bytes 1916932
  634.8 28.9 %collective-permute-start.17 = (bf16[416,768]{1,0:T(8,128)(2,1)}, bf16[416,768]{1,0:T(8,128)(2,1)S(1)}, u32[]{:S(2)}, u32[]{:S(2)}) collective-permute-start(bf16[416,768]{1,0:T(8,128)(2,1)} %collective-permute-done.16.refs_1_), channel_id=1, source_target_pairs={{0,1},{1,0},{2,3},{3,2},{4,5},{5,4},{6,7},{7,6},{8,9},{9,8},{10,11... | collective-permute-start | bytes 1916936 | tf_op jit(solution)/shard_map/ppermute | solution.py:356
  634.9 20.1 %copy-start.33 = (f32[8,768]{1,0:T(8,128)S(1)}, f32[8,768]{1,0:T(8,128)}, u32[]{:S(2)}) copy-start(f32[8,768]{1,0:T(8,128)} %get-tuple-element.38) | copy-start | bytes 73732
  634.9 28.8 %collective-permute-start.19 = (bf16[416,768]{1,0:T(8,128)(2,1)S(1)}, bf16[416,768]{1,0:T(8,128)(2,1)S(1)}, u32[]{:S(2)}, u32[]{:S(2)}) collective-permute-start(bf16[416,768]{1,0:T(8,128)(2,1)S(1)} %collective-permute-done.18.refs_3_), channel_id=1, source_target_pairs={{0,1},{1,0},{2,3},{3,2},{4,5},{5,4},{6,7},{7,6},{8,9},{9,8},{10,11... | collective-permute-start | bytes 1916936 | tf_op jit(solution)/shard_map/ppermute | solution.py:356
  654.5 8.4 collective-permute-start.32
  654.9 9.7 %collective-permute-start.21 = (bf16[416,768]{1,0:T(8,128)(2,1)S(1)}, bf16[416,768]{1,0:T(8,128)(2,1)}, u32[]{:S(2)}, u32[]{:S(2)}) collective-permute-start(bf16[416,768]{1,0:T(8,128)(2,1)S(1)} %collective-permute-done.20.refs_5_), channel_id=1, source_target_pairs={{0,1},{1,0},{2,3},{3,2},{4,5},{5,4},{6,7},{7,6},{8,9},{9,8},{10,11... | collective-permute-start | bytes 1916936 | tf_op jit(solution)/shard_map/ppermute | solution.py:356
  846.0 16.3 %copy-start.29 = (bf16[768,128]{1,0:T(8,128)(2,1)S(1)}, bf16[768,128]{1,0:T(8,128)(2,1)}, u32[]{:S(2)}) copy-start(bf16[768,128]{1,0:T(8,128)(2,1)} %get-tuple-element.45) | copy-start | bytes 589828
  846.0 16.3 %copy-start.28 = (bf16[768,128]{1,0:T(8,128)(2,1)S(1)}, bf16[768,128]{1,0:T(8,128)(2,1)}, u32[]{:S(2)}) copy-start(bf16[768,128]{1,0:T(8,128)(2,1)} %get-tuple-element.46) | copy-start | bytes 589828
  870.1 18.6 %copy-start.15 = (bf16[96,1920]{1,0:T(8,128)(2,1)S(1)}, bf16[96,1920]{1,0:T(8,128)(2,1)}, u32[]{:S(2)}) copy-start(bf16[96,1920]{1,0:T(8,128)(2,1)} %add_convert_fusion.6) | copy-start | bytes 1105924
  870.1 18.6 %copy-start.13 = (bf16[768,1152]{1,0:T(8,128)(2,1)S(1)}, bf16[768,1152]{1,0:T(8,128)(2,1)}, u32[]{:S(2)}) copy-start(bf16[768,1152]{1,0:T(8,128)(2,1)} %place.5) | copy-start | bytes 5308420
  870.4 36.5 %collective-permute-start.23 = (bf16[208,1152]{1,0:T(8,128)(2,1)S(1)}, bf16[208,1152]{1,0:T(8,128)(2,1)S(1)}, u32[]{:S(2)}, u32[]{:S(2)}) collective-permute-start(bf16[208,1152]{1,0:T(8,128)(2,1)S(1)} %get-tuple-element.109), channel_id=1, source_target_pairs={{0,8},{8,0},{16,24},{24,16},{1,9},{9,1},{17,25},{25,17},{2,10},{10... | collective-permute-start | bytes 1437704 | tf_op jit(solution)/shard_map/ppermute | solution.py:353
  870.5 38.5 %collective-permute-start.24 = (bf16[208,1152]{1,0:T(8,128)(2,1)S(1)}, bf16[208,1152]{1,0:T(8,128)(2,1)S(1)}, u32[]{:S(2)}, u32[]{:S(2)}) collective-permute-start(bf16[208,1152]{1,0:T(8,128)(2,1)S(1)} %get-tuple-element.110), channel_id=1, source_target_pairs={{0,16},{8,24},{16,0},{24,8},{1,17},{9,25},{17,1},{25,9},{2,18},{10... | collective-permute-start | bytes 1437704 | tf_op jit(solution)/shard_map/ppermute | solution.py:353
  878.1 30.8 %copy-start.27 = (f32[6,1152]{1,0:T(8,128)S(1)}, f32[6,1152]{1,0:T(8,128)}, u32[]{:S(2)}) copy-start(f32[6,1152]{1,0:T(8,128)} %reshape.88) | copy-start | bytes 82948
  878.1 30.8 %collective-permute-start.25 = (bf16[208,1152]{1,0:T(8,128)(2,1)S(1)}, bf16[208,1152]{1,0:T(8,128)(2,1)S(1)}, u32[]{:S(2)}, u32[]{:S(2)}) collective-permute-start(bf16[208,1152]{1,0:T(8,128)(2,1)S(1)} %get-tuple-element.111), channel_id=1, source_target_pairs={{0,24},{8,16},{16,8},{24,0},{1,25},{9,17},{17,9},{25,1},{2,26},{10... | collective-permute-start | bytes 1437704 | tf_op jit(solution)/shard_map/ppermute | solution.py:353
  878.1 20.8 %collective-permute-start.39 = (bf16[96,1536]{1,0:T(8,128)(2,1)S(1)}, bf16[96,1536]{1,0:T(8,128)(2,1)S(1)}, u32[]{:S(2)}, u32[]{:S(2)}) collective-permute-start(bf16[96,1536]{1,0:T(8,128)(2,1)S(1)} %copy-done.16), channel_id=1, source_target_pairs={{0,4},{2,6},{4,0},{6,2},{1,5},{3,7},{5,1},{7,3},{8,12},{10,14},{12... | collective-permute-start | bytes 884744 | tf_op jit(solution)/shard_map/ppermute | solution.py:353
  888.7 18.1 %collective-permute-start.33 = (bf16[96,1920]{1,0:T(8,128)(2,1)S(1)}, bf16[96,1920]{1,0:T(8,128)(2,1)S(1)}, u32[]{:S(2)}, u32[]{:S(2)}) collective-permute-start(bf16[96,1920]{1,0:T(8,128)(2,1)S(1)} %copy-done.15), channel_id=1, source_target_pairs={{0,4},{2,6},{4,0},{6,2},{1,5},{3,7},{5,1},{7,3},{8,12},{10,14},{12... | collective-permute-start | bytes 1105928 | tf_op jit(solution)/shard_map/ppermute | solution.py:353
  898.9 46.7 %collective-permute-start.22 = (bf16[768,768]{1,0:T(8,128)(2,1)}, bf16[768,768]{1,0:T(8,128)(2,1)}, u32[]{:S(2)}, u32[]{:S(2)}) collective-permute-start(bf16[768,768]{1,0:T(8,128)(2,1)} %convolution_convert_fusion.4), channel_id=1, source_target_pairs={{0,1},{1,0},{2,3},{3,2},{4,5},{5,4},{6,7},{7,6},{8,9},{9,8},{10,11... | collective-permute-start | bytes 3538952 | tf_op jit(solution)/shard_map/ppermute | solution.py:356
  906.7 9.9 %collective-permute-start.40 = (bf16[96,1536]{1,0:T(8,128)(2,1)S(1)}, bf16[96,1536]{1,0:T(8,128)(2,1)S(1)}, u32[]{:S(2)}, u32[]{:S(2)}) collective-permute-start(bf16[96,1536]{1,0:T(8,128)(2,1)S(1)} %add_convert_fusion.7), channel_id=1, source_target_pairs={{0,2},{2,0},{4,6},{6,4},{1,3},{3,1},{5,7},{7,5},{8,10},{10,8},{12,... | collective-permute-start | bytes 884744 | tf_op jit(solution)/shard_map/ppermute | solution.py:353
  906.8 22.5 %collective-permute-start.34 = (bf16[96,1920]{1,0:T(8,128)(2,1)S(1)}, bf16[96,1920]{1,0:T(8,128)(2,1)S(1)}, u32[]{:S(2)}, u32[]{:S(2)}) collective-permute-start(bf16[96,1920]{1,0:T(8,128)(2,1)S(1)} %add_convert_fusion.5), channel_id=1, source_target_pairs={{0,2},{2,0},{4,6},{6,4},{1,3},{3,1},{5,7},{7,5},{8,10},{10,8},{12,... | collective-permute-start | bytes 1105928 | tf_op jit(solution)/shard_map/ppermute | solution.py:353
  909.3 19.8 %collective-permute-start.26 = (bf16[112,1152]{1,0:T(8,128)(2,1)S(1)}, bf16[112,1152]{1,0:T(8,128)(2,1)S(1)}, u32[]{:S(2)}, u32[]{:S(2)}) collective-permute-start(bf16[112,1152]{1,0:T(8,128)(2,1)S(1)} %pad_maximum_fusion.15), channel_id=1, source_target_pairs={{0,2},{2,0},{4,6},{6,4},{1,3},{3,1},{5,7},{7,5},{8,10},{10,8},{12,... | collective-permute-start | bytes 774152 | tf_op jit(solution)/shard_map/ppermute | solution.py:353
  929.2 13.8 %collective-permute-start.27 = (bf16[112,1152]{1,0:T(8,128)(2,1)S(1)}, bf16[112,1152]{1,0:T(8,128)(2,1)S(1)}, u32[]{:S(2)}, u32[]{:S(2)}) collective-permute-start(bf16[112,1152]{1,0:T(8,128)(2,1)S(1)} %pad_maximum_fusion.14), channel_id=1, source_target_pairs={{0,4},{2,6},{4,0},{6,2},{1,5},{3,7},{5,1},{7,3},{8,12},{10,14},{12... | collective-permute-start | bytes 774152 | tf_op jit(solution)/shard_map/ppermute | solution.py:353
  929.4 16.2 %copy-start.1 = (f32[768,768]{1,0:T(8,128)S(1)}, f32[768,768]{1,0:T(8,128)}, u32[]{:S(2)}) copy-start(f32[768,768]{1,0:T(8,128)} %copy-done) | copy-start | bytes 7077892
  945.5 7.4 collective-permute-start.28
  (34 other events, 191.5 us)
